TPU v7x, 32 devices: a whole 2x2x4 slice. The times are simulated.
32 devices in a mesh: dp: 8 (over y, x, core), expert: 4 (over z).
Axes of the slice: x: 2, y: 2, z: 4, core: 2. Of those that a mesh axis runs over, the one named last changes fastest.
Arguments:
- tokens: bfloat16 [4096, 1280], P(('dp', 'expert')), may hold values from -6 to 6
- cotangent: bfloat16 [4096, 1280], P(('dp', 'expert')), may hold values from -4 to 4
- gate_weights: float32 [4096, 2], P(('dp', 'expert')), may hold values from 0.1 to 1
- expert_ids: int32 [4096, 2], P(('dp', 'expert')), may hold values from 0 to 7, as said below
- segments: int32 [32, 128], P(('dp', 'expert')), may hold values from 0 to 3, never falling along the last dimension, each value on 1 to 64 neighbouring positions
- keep_counts: int32 [32, 4], P(('dp', 'expert')), may hold values from 1 to 64
- expand_weight: bfloat16 [8, 2560, 1280], P('expert', 'dp'), may hold values from -0.15625 to 0.15625
- reduce_weight: bfloat16 [8, 2560, 1280], P('expert', 'dp'), may hold values from -0.125 to 0.125
Outputs:
- output: bfloat16 [4096, 1280], P(('dp', 'expert'))
- tokens_grad: bfloat16 [4096, 1280], P(('dp', 'expert'))
- gating_grad: float32 [4096, 2], P(('dp', 'expert'))
- expand_grad: bfloat16 [8, 2560, 1280], P('expert', 'dp')
- reduce_grad: bfloat16 [8, 2560, 1280], P('expert', 'dp')
Inputs may be any that keep to these rules, and one draw needn't show every extreme that they name: `expert_ids`: the 128 tokens of one sequence name each expert exactly 32 times, and a token's 2 experts differ. `segments`: within a sequence the ids never fall, every image 0 to 3 appears, each holds 1 to 64 positions.
All inputs are finite; a program needn't handle non-finite values.
Results may differ from a plain program's by a relative error of at most 0.015.
Values may be sent and summed in bfloat16 or wider, within the bound.
No kernel may reach another device: no remote copies, remote signals or barrier semaphores. Data moves between devices by JAX's collectives and lax.ppermute only.
A program may use at most 128 MiB of HBM per device.

v0:
```python
import functools

import jax
import jax.numpy as jnp
from jax import lax
from jax.experimental import pallas as pl
from jax.experimental.pallas import tpu as pltpu
from jax.sharding import PartitionSpec as P

epsilon = 1e-06
root_half = 0.7071067811865476
density_scale = 0.3989422804014327


def dot(left, right, left_dim, right_dim):
    return lax.dot_general(
        left, right, (((left_dim,), (right_dim,)), ((), ())), preferred_element_type=jnp.float32
    )


def normalize(tokens):
    wide = tokens.astype(jnp.float32)
    centred = wide - jnp.mean(wide, axis=1, keepdims=True)
    inv_scale = lax.rsqrt(jnp.mean(centred * centred, axis=1, keepdims=True) + epsilon)
    return centred * inv_scale, inv_scale


def one_hot(target, rows):
    lanes = lax.broadcasted_iota(jnp.int32, (target.shape[0], rows), 1)
    return (target == lanes).astype(jnp.bfloat16)


def to_column(row, same):
    return jnp.sum(jnp.where(same, row, 0.0), axis=1, keepdims=True)


def route_kernel(
    planes, local, me_ref, tok_hbm, cot_hbm, gate_ref, ids_ref, seg_ref, keep_ref, *refs
):
    outs, (tok_ref, cot_ref, sems) = refs[:-3], refs[-3:]
    tok_copy = pltpu.make_async_copy(tok_hbm, tok_ref, sems.at[0])
    cot_copy = pltpu.make_async_copy(cot_hbm, cot_ref, sems.at[1])
    tok_copy.start()
    cot_copy.start()
    top, toks = ids_ref.shape
    experts = planes * local
    cap = top * toks // experts
    feature_refs = [outs[l * planes : (l + 1) * planes] for l in range(local)]
    grad_refs = outs[local * planes : (local + 1) * planes]
    target_ref, weight_ref, alive_ref = outs[(local + 1) * planes :]
    seg = seg_ref[...]
    spot = lax.broadcasted_iota(jnp.int32, seg.shape, 1).astype(jnp.float32)
    alive_row = jnp.zeros(seg.shape, jnp.float32)
    for image in range(keep_ref.shape[1]):
        start = jnp.sum((seg < image).astype(jnp.float32), axis=1, keepdims=True)
        limit = keep_ref[0:1, image : image + 1].astype(jnp.float32)
        alive_row = jnp.where((seg == image) & (spot - start < limit), 1.0, alive_row)
    row = lax.broadcasted_iota(jnp.int32, (toks, toks), 0)
    col = lax.broadcasted_iota(jnp.int32, (toks, toks), 1)
    same = row == col
    alive = to_column(alive_row, same)
    width = -(-experts // 128) * 128
    lanes = lax.broadcasted_iota(jnp.int32, (toks, width), 1)
    picks = [
        to_column(ids_ref[k : k + 1, :].astype(jnp.float32), same).astype(jnp.int32)
        for k in range(top)
    ]
    chosen = [(pick == lanes).astype(jnp.float32) for pick in picks]
    every = chosen[0]
    for k in range(1, top):
        every = every + chosen[k]
    before = dot((col < row).astype(jnp.bfloat16), every.astype(jnp.bfloat16), 1, 0)
    me = me_ref[0]
    hots = []
    weights = []
    for k in range(top):
        slot = jnp.sum(before * chosen[k], axis=1, keepdims=True).astype(jnp.int32)
        away = jnp.bitwise_xor(lax.div(picks[k], local), me)
        target = (away * local + lax.rem(picks[k], local)) * cap + slot
        weight = to_column(gate_ref[k : k + 1, :] * alive_row, same)
        target_ref[:, k : k + 1] = target
        weight_ref[:, k : k + 1] = weight
        hots.append(one_hot(target, experts * cap))
        weights.append(weight)
    alive_ref[...] = alive
    tok_copy.wait()
    normed, _ = normalize(tok_ref[...])
    low = jnp.where(alive > 0, normed, 0.0).astype(jnp.bfloat16)
    every_hot = hots[0]
    for k in range(1, top):
        every_hot = every_hot + hots[k]
    features = dot(every_hot, low, 0, 0).astype(jnp.bfloat16)
    for away in range(planes):
        base = away * local * cap
        for l in range(local):
            feature_refs[l][away][...] = features[base + l * cap : base + (l + 1) * cap]
    cot_copy.wait()
    cot = cot_ref[...].astype(jnp.float32)
    scaled = [(cot * weight).astype(jnp.bfloat16) for weight in weights]
    grads = dot(jnp.concatenate(hots, 0), jnp.concatenate(scaled, 0), 0, 0).astype(jnp.bfloat16)
    for away in range(planes):
        base = away * local * cap
        grad_refs[away][...] = grads[base : base + local * cap]


def join_kernel(planes, cap, *refs):
    piece_refs, outs = refs[:planes], refs[planes:]
    for l, out in enumerate(outs):
        for away, ref in enumerate(piece_refs):
            out[away * cap : (away + 1) * cap] = ref[l * cap : (l + 1) * cap]


def add_kernel(*refs):
    total = refs[0][0].astype(jnp.float32)
    for ref in refs[1:-1]:
        total = total + ref[0].astype(jnp.float32)
    refs[-1][0] = total.astype(jnp.bfloat16)


def forward_kernel(blocks, parts, *refs):
    rows_refs = refs[:blocks]
    up_own, up_pair, down_own, down_pair, hidden_ref, slope_ref = refs[blocks : blocks + 6]
    rows = jnp.concatenate([ref[...] for ref in rows_refs], 0)
    up = jnp.concatenate([up_own[0], up_pair[0]], 0)
    pre = dot(rows, up, 1, 1)
    half = 0.5 * (1.0 + lax.erf(pre * root_half))
    hidden = (pre * half).astype(jnp.bfloat16)
    hidden_ref[...] = hidden
    slope_ref[...] = half + pre * jnp.exp(-0.5 * pre * pre) * density_scale
    down = jnp.concatenate([down_own[0], down_pair[0]], 0)
    spread(dot(hidden, down, 1, 0), blocks, parts, refs[blocks + 6 :])


def spread(result, blocks, parts, refs):
    block_rows = result.shape[0] // blocks
    for number, (start, stop, slots) in enumerate(parts):
        for index, pair in enumerate(slots):
            for ref, block in zip(refs[2 * number : 2 * number + 2], pair):
                base = block * block_rows
                ref[index] = result[base + start : base + stop].astype(jnp.bfloat16)


def backward_kernel(blocks, parts, *refs):
    grad_refs = refs[:blocks]
    up_own, up_pair, down_own, down_pair, slope_ref, dpre_ref = refs[blocks : blocks + 6]
    grads = jnp.concatenate([ref[...] for ref in grad_refs], 0)
    down = jnp.concatenate([down_own[0], down_pair[0]], 0)
    dpre = (dot(grads, down, 1, 1) * slope_ref[...]).astype(jnp.bfloat16)
    dpre_ref[...] = dpre
    up = jnp.concatenate([up_own[0], up_pair[0]], 0)
    spread(dot(dpre, up, 1, 0), blocks, parts, refs[blocks + 6 :])


def weight_kernel(blocks, *refs):
    rows_refs = refs[:blocks]
    grad_refs = refs[blocks : 2 * blocks]
    hidden_ref, dpre_ref, own_ref, pair_ref = refs[2 * blocks :]
    units = own_ref.shape[1]
    for index, (left_ref, right_refs) in enumerate(
        ((dpre_ref, rows_refs), (hidden_ref, grad_refs))
    ):
        right = jnp.concatenate([ref[...] for ref in right_refs], 0)
        product = dot(left_ref[...], right, 0, 0)
        own_ref[index] = product[:units].astype(jnp.bfloat16)
        pair_ref[index] = product[units:].astype(jnp.bfloat16)


def total_kernel(local, *refs):
    own_refs = refs[:local]
    pair_refs = refs[local : 2 * local]
    out_refs = refs[2 * local :]
    for l in range(local):
        for index, ref in enumerate(out_refs):
            ref[l] = (
                own_refs[l][index].astype(jnp.float32) + pair_refs[l][index].astype(jnp.float32)
            ).astype(jnp.bfloat16)


def finish_kernel(groups, *refs):
    outs = refs[sum(count for counts in groups for count in counts) :]
    cap = outs[0].shape[0] // len(groups)
    used = 0
    for l, counts in enumerate(groups):
        away = 0
        for count in counts:
            total = refs[used][0].astype(jnp.float32)
            for ref in refs[used + 1 : used + count]:
                total = total + ref[0].astype(jnp.float32)
            used += count
            low = total.astype(jnp.bfloat16)
            for index in range(low.shape[0] // cap):
                outs[away][l * cap : (l + 1) * cap] = low[index * cap : (index + 1) * cap]
                away += 1


def output_kernel(planes, *refs):
    result_refs = refs[:planes]
    tok_ref, cot_ref, target_ref, weight_ref, alive_ref, out_ref, gating_ref = refs[planes:]
    results = jnp.concatenate([ref[...] for ref in result_refs], 0)
    toks = tok_ref.shape[0]
    row = lax.broadcasted_iota(jnp.int32, (toks, toks), 0)
    same = row == lax.broadcasted_iota(jnp.int32, (toks, toks), 1)
    total = tok_ref[...].astype(jnp.float32)
    cot = cot_ref[...].astype(jnp.float32)
    for k in range(target_ref.shape[1]):
        picked = dot(one_hot(target_ref[:, k : k + 1], results.shape[0]), results, 1, 0)
        total = total + weight_ref[:, k : k + 1] * picked
        column = alive_ref[...] * jnp.sum(cot * picked, axis=1, keepdims=True)
        gating_ref[k : k + 1, :] = jnp.sum(jnp.where(same, column, 0.0), axis=0, keepdims=True)
    out_ref[...] = total.astype(jnp.bfloat16)


def input_kernel(planes, local, *refs):
    grad_refs = refs[: planes * local]
    tok_ref, cot_ref, target_ref, alive_ref, out_ref = refs[planes * local :]
    grads = jnp.concatenate([ref[...] for ref in grad_refs], 0)
    hot = one_hot(target_ref[:, 0:1], grads.shape[0])
    for k in range(1, target_ref.shape[1]):
        hot = hot + one_hot(target_ref[:, k : k + 1], grads.shape[0])
    dnorm = alive_ref[...] * dot(hot, grads, 1, 0)
    normed, inv_scale = normalize(tok_ref[...])
    inner = jnp.mean(dnorm * normed, axis=1, keepdims=True)
    change = dnorm - jnp.mean(dnorm, axis=1, keepdims=True) - normed * inner
    out_ref[...] = (cot_ref[...].astype(jnp.float32) + inv_scale * change).astype(jnp.bfloat16)


def whole(array):
    rank = len(array.shape)
    return pl.BlockSpec(array.shape, lambda *_: (0,) * rank)


def part(array, index):
    rank = len(array.shape)
    return pl.BlockSpec((1,) + array.shape[1:], lambda *_: (index,) + (0,) * (rank - 1))


def run(kernel, inputs, outs):
    arrays = [item[0] if isinstance(item, tuple) else item for item in inputs]
    specs = [part(*item) if isinstance(item, tuple) else whole(item) for item in inputs]
    outs = [jax.ShapeDtypeStruct(shape, dtype) for shape, dtype in outs]
    return pl.pallas_call(
        kernel,
        out_shape=outs,
        grid=(1,),
        in_specs=specs,
        out_specs=[whole(out) for out in outs],
        compiler_params=pltpu.CompilerParams(vmem_limit_bytes=40 << 20),
    )(*arrays)


def body(
    tokens, cotangent, gate_weights, expert_ids, segments, keep_counts, expand_weight, reduce_weight
):
    toks, width = tokens.shape
    top = expert_ids.shape[1]
    groups = lax.axis_size("dp")
    planes = lax.axis_size("expert")
    local, units, _ = expand_weight.shape
    cap = top * toks // (planes * local)
    blocks = groups // 2
    bits = [1 << bit for bit in range(1, groups.bit_length() - 1)]
    block_rows = planes * cap
    low = jnp.bfloat16

    def swap(values, mask):
        return lax.ppermute(values, "dp", [(i, i ^ mask) for i in range(groups)])

    def cross(pieces):
        away = []
        for s in range(1, planes):
            away.append(
                lax.ppermute(pieces[s], "expert", [(i, i ^ s) for i in range(planes)])
            )
        return [pieces[0]] + away

    def order_of(index):
        shift = index % len(bits)
        return bits[shift:] + bits[:shift]

    def gather(own, order):
        held = {0: own}
        for bit in order:
            for block in sorted(held):
                held[block | bit] = swap(held[block], bit)
        return [held[2 * index] for index in range(blocks)]

    def part_of(start, stop, order):
        bit = order[0] // 2
        slots = tuple((block | bit, block) for block in range(blocks) if not block & bit)
        return start, stop, slots

    def scatter(send, keep, order):
        bit = order[0]
        arrived = swap(send, bit)
        terms = {
            2 * slots[1]: [(keep, index), (arrived, index)]
            for index, slots in enumerate(part_of(0, 0, order)[2])
        }
        for bit in order[1:]:
            leaving = [block for block in sorted(terms) if block & bit]
            sums = [
                run(add_kernel, terms[block], [((1,) + send.shape[1:], low)])[0]
                for block in leaving
            ]
            sums = sums[0] if len(sums) == 1 else jnp.concatenate(sums, 0)
            arrived = swap(sums, bit)
            for index, block in enumerate(leaving):
                terms[block ^ bit].append((arrived, index))
                del terms[block]
        return terms[0]

    me = lax.axis_index("expert").astype(jnp.int32).reshape(1)
    routed = pl.pallas_call(
        functools.partial(route_kernel, planes, local),
        out_shape=[jax.ShapeDtypeStruct((cap, width), low)] * (local * planes)
        + [jax.ShapeDtypeStruct((local * cap, width), low)] * planes
        + [
            jax.ShapeDtypeStruct((toks, top), jnp.int32),
            jax.ShapeDtypeStruct((toks, top), jnp.float32),
            jax.ShapeDtypeStruct((toks, 1), jnp.float32),
        ],
        in_specs=[pl.BlockSpec(memory_space=pltpu.SMEM)]
        + [pl.BlockSpec(memory_space=pltpu.HBM)] * 2
        + [pl.BlockSpec(memory_space=pltpu.VMEM)] * 4,
        scratch_shapes=[
            pltpu.VMEM(tokens.shape, tokens.dtype),
            pltpu.VMEM(tokens.shape, tokens.dtype),
            pltpu.SemaphoreType.DMA((2,)),
        ],
        compiler_params=pltpu.CompilerParams(vmem_limit_bytes=40 << 20),
        name="route",
    )(me, tokens, cotangent, gate_weights.T, expert_ids.T, segments, keep_counts)
    target, weight, alive = routed[-3:]
    up_pair = swap(expand_weight, 1)
    down_pair = swap(reduce_weight, 1)

    features = []
    for l in range(local):
        pieces = cross(routed[l * planes : (l + 1) * planes])
        (own,) = run(
            functools.partial(join_kernel, planes, cap), pieces, [((block_rows, width), low)]
        )
        features.append(gather(own, order_of(l)))
    pieces = cross(routed[local * planes : (local + 1) * planes])
    owns = run(
        functools.partial(join_kernel, planes, cap), pieces, [((block_rows, width), low)] * local
    )
    grads = [gather(owns[l], order_of(l)) for l in range(local)]

    rows = blocks * block_rows

    def outs_of(parts):
        return [
            ((blocks // 2, stop - start, width), low) for start, stop, _ in parts for _ in range(2)
        ]

    hiddens, slopes, result_terms = [], [], []
    for l in range(local):
        parts = [part_of(0, block_rows, order_of(l))]
        hidden, slope, send, keep = run(
            functools.partial(forward_kernel, blocks, parts),
            features[l]
            + [(expand_weight, l), (up_pair, l), (reduce_weight, l), (down_pair, l)],
            [((rows, 2 * units), low), ((rows, 2 * units), jnp.float32)] + outs_of(parts),
        )
        hiddens.append(hidden)
        slopes.append(slope)
        result_terms.append([scatter(send, keep, order_of(l))])
    half = block_rows // 2
    dpres, input_terms = [], []
    for l in range(local):
        parts = [part_of(0, half, order_of(0)), part_of(half, block_rows, order_of(1))]
        dpre, *sends = run(
            functools.partial(backward_kernel, blocks, parts),
            grads[l]
            + [(expand_weight, l), (up_pair, l), (reduce_weight, l), (down_pair, l), slopes[l]],
            [((rows, 2 * units), low)] + outs_of(parts),
        )
        dpres.append(dpre)
        input_terms.append(
            [scatter(sends[2 * index], sends[2 * index + 1], order_of(index)) for index in range(2)]
        )
    owns, pairs = [], []
    for l in range(local):
        own, pair = run(
            functools.partial(weight_kernel, blocks),
            features[l] + grads[l] + [hiddens[l], dpres[l]],
            [((2, units, width), low)] * 2,
        )
        owns.append(own)
        pairs.append(swap(pair, 1))
    expand_grad, reduce_grad = run(
        functools.partial(total_kernel, local), owns + pairs, [(expand_weight.shape, low)] * 2
    )

    def finish(terms_list):
        groups = [[len(terms) for terms in parts] for parts in terms_list]
        outs = run(
            functools.partial(finish_kernel, groups),
            [item for parts in terms_list for terms in parts for item in terms],
            [((len(terms_list) * cap, width), low)] * planes,
        )
        return cross(outs)

    returned = finish(result_terms)
    output, gating_grad = run(
        functools.partial(output_kernel, planes),
        returned + [tokens, cotangent, target, weight, alive],
        [(tokens.shape, low), ((top, toks), jnp.float32)],
    )
    back = [finish([input_terms[l]]) for l in range(local)]
    (tokens_grad,) = run(
        functools.partial(input_kernel, planes, local),
        [back[l][s] for s in range(planes) for l in range(local)]
        + [tokens, cotangent, target, alive],
        [(tokens.shape, low)],
    )
    return (output, tokens_grad, gating_grad.T, expand_grad, reduce_grad)


def solution(mesh):
    rows = P(("dp", "expert"), None)
    weights = P("expert", "dp", None)

    return jax.shard_map(
        body,
        mesh=mesh,
        in_specs=(rows,) * 6 + (weights,) * 2,
        out_specs=(rows,) * 3 + (weights,) * 2,
        check_vma=False,
    )
```

profile of v0, /device:TPU:0, one launch (start us, length us, event | category | flops | bytes accessed | tf_op | source)
XLA Modules:
  0.0 193.7 jit_solution(6907368189241969272)
XLA Ops:
  5.9 1.6 route.1
  7.5 3.1 %collective-permute-start = (bf16[32,1280]{1,0:T(8,128)(2,1)S(1)}, bf16[32,1280]{1,0:T(8,128)(2,1)S(1)}, u32[]{:S(2)}, u32[]{:S(2)}) collective-permute-start(bf16[32,1280]{1,0:T(8,128)(2,1)S(1)} %get-tuple-element.61), channel_id=1, source_target_pairs={{0,1},{1,0},{2,3},{3,2},{4,5},{5,4},{6,7},{7,6},{8,9},{9,8},{10,11... | collective-permute-start | bytes 245768 | tf_op jit(solution)/shard_map/ppermute | solution.py:272
  10.6 2.6 %collective-permute-start.1 = (bf16[32,1280]{1,0:T(8,128)(2,1)S(1)}, bf16[32,1280]{1,0:T(8,128)(2,1)S(1)}, u32[]{:S(2)}, u32[]{:S(2)}) collective-permute-start(bf16[32,1280]{1,0:T(8,128)(2,1)S(1)} %get-tuple-element.62), channel_id=1, source_target_pairs={{0,2},{1,3},{2,0},{3,1},{4,6},{5,7},{6,4},{7,5},{8,10},{9,11},{10,... | collective-permute-start | bytes 245768 | tf_op jit(solution)/shard_map/ppermute | solution.py:272
  13.2 1.8 collective-permute-start.10
  15.0 5.4 %collective-permute-done.1.refs_2_ = bf16[32,1280]{1,0:T(8,128)(2,1)S(1)} collective-permute-done((bf16[32,1280]{1,0:T(8,128)(2,1)S(1)}, bf16[32,1280]{1,0:T(8,128)(2,1)S(1)}, u32[]{:S(2)}, u32[]{:S(2)}) %collective-permute-start.1) | collective-permute-done | bytes 81952 | tf_op jit(solution)/shard_map/ppermute | solution.py:272
  20.4 3.8 %collective-permute-start.21 = (bf16[64,1280]{1,0:T(8,128)(2,1)S(1)}, bf16[64,1280]{1,0:T(8,128)(2,1)S(1)}, u32[]{:S(2)}, u32[]{:S(2)}) collective-permute-start(bf16[64,1280]{1,0:T(8,128)(2,1)S(1)} %get-tuple-element.81), channel_id=1, source_target_pairs={{0,1},{1,0},{2,3},{3,2},{4,5},{5,4},{6,7},{7,6},{8,9},{9,8},{10,11... | collective-permute-start | bytes 491528 | tf_op jit(solution)/shard_map/ppermute | solution.py:272
  24.2 1.5 collective-permute-start.12
  27.8 2.9 %collective-permute-done.12.refs_3_ = bf16[32,1280]{1,0:T(8,128)(2,1)S(1)} collective-permute-done((bf16[32,1280]{1,0:T(8,128)(2,1)S(1)}, bf16[32,1280]{1,0:T(8,128)(2,1)S(1)}, u32[]{:S(2)}, u32[]{:S(2)}) %collective-permute-start.12) | collective-permute-done | bytes 81952 | tf_op jit(solution)/shard_map/ppermute | solution.py:272
  32.2 8.9 %collective-permute-done.22.refs_2_ = bf16[64,1280]{1,0:T(8,128)(2,1)S(1)} collective-permute-done((bf16[64,1280]{1,0:T(8,128)(2,1)S(1)}, bf16[64,1280]{1,0:T(8,128)(2,1)S(1)}, u32[]{:S(2)}, u32[]{:S(2)}) %collective-permute-start.22) | collective-permute-done | bytes 163872 | tf_op jit(solution)/shard_map/ppermute | solution.py:272
  41.0 1.5 collective-permute-start.4
  43.2 1.6 collective-permute-start.24
  44.8 6.8 %collective-permute-done.4.refs_2_ = bf16[128,1280]{1,0:T(8,128)(2,1)S(1)} collective-permute-done((bf16[128,1280]{1,0:T(8,128)(2,1)S(1)}, bf16[128,1280]{1,0:T(8,128)(2,1)S(1)}, u32[]{:S(2)}, u32[]{:S(2)}) %collective-permute-start.4) | collective-permute-done | bytes 327712 | tf_op jit(solution)/shard_map/ppermute | solution.py:266
  51.6 1.5 collective-permute-start.25
  53.1 5.5 %collective-permute-done.14.refs_2_ = bf16[128,1280]{1,0:T(8,128)(2,1)S(1)} collective-permute-done((bf16[128,1280]{1,0:T(8,128)(2,1)S(1)}, bf16[128,1280]{1,0:T(8,128)(2,1)S(1)}, u32[]{:S(2)}, u32[]{:S(2)}) %collective-permute-start.14) | collective-permute-done | bytes 327712 | tf_op jit(solution)/shard_map/ppermute | solution.py:266
  58.6 1.5 collective-permute-start.32
  60.7 5.0 %collective-permute-done.25.refs_2_.refs_6_ = bf16[128,1280]{1,0:T(8,128)(2,1)S(1)} collective-permute-done((bf16[128,1280]{1,0:T(8,128)(2,1)S(1)}, bf16[128,1280]{1,0:T(8,128)(2,1)S(1)}, u32[]{:S(2)}, u32[]{:S(2)}) %collective-permute-start.25) | collective-permute-done | bytes 327712 | tf_op jit(solution)/shard_map/ppermute | solution.py:266
  65.6 1.5 collective-permute-start.26
  67.2 5.5 %collective-permute-done.32.refs_2_.refs_6_ = bf16[128,1280]{1,0:T(8,128)(2,1)S(1)} collective-permute-done((bf16[128,1280]{1,0:T(8,128)(2,1)S(1)}, bf16[128,1280]{1,0:T(8,128)(2,1)S(1)}, u32[]{:S(2)}, u32[]{:S(2)}) %collective-permute-start.32) | collective-permute-done | bytes 327712 | tf_op jit(solution)/shard_map/ppermute | solution.py:266
  74.2 5.5 %collective-permute-done.5.refs_3_ = bf16[128,1280]{1,0:T(8,128)(2,1)S(1)} collective-permute-done((bf16[128,1280]{1,0:T(8,128)(2,1)S(1)}, bf16[128,1280]{1,0:T(8,128)(2,1)S(1)}, u32[]{:S(2)}, u32[]{:S(2)}) %collective-permute-start.5) | collective-permute-done | bytes 327712 | tf_op jit(solution)/shard_map/ppermute | solution.py:266
  81.7 1.5 collective-permute-start.33
  84.6 3.7 %shard_map.120 = (bf16[512,640]{1,0:T(8,128)(2,1)S(1)}, f32[512,640]{1,0:T(8,128)S(1)}, bf16[2,128,1280]{2,1,0:T(8,128)(2,1)S(1)}, bf16[2,128,1280]{2,1,0:T(8,128)(2,1)S(1)}) custom-call(bf16[128,1280]{1,0:T(8,128)(2,1)S(1)} %shard_map.119.refs_0_, bf16[128,1280]{1,0:T(8,128)(2,1)S(1)} %collective-permute-done.3.refs_1_, ...), custom_call_target="tpu_custom_call" | custom-call | tf_op jit(solution)/shard_map/pallas_call | solution.py:241
  88.3 4.2 %shard_map.128 = (bf16[512,640]{1,0:T(8,128)(2,1)S(1)}, bf16[2,64,1280]{2,1,0:T(8,128)(2,1)}, bf16[2,64,1280]{2,1,0:T(8,128)(2,1)S(1)}, bf16[2,64,1280]{2,1,0:T(8,128)(2,1)S(1)}, bf16[2,64,1280]{2,1,0:T(8,128)(2,1)S(1)}) custom-call(bf16[128,1280]{1,0:T(8,128)(2,1)S(1)} %get-tuple-element.84.refs_0_.refs_4_, ...), custom_call_target="tpu_custom_call" | custom-call | tf_op jit(solution)/shard_map/pallas_call | solution.py:241
  93.1 1.5 collective-permute-start.29
  94.6 3.1 %shard_map.137 = (bf16[2,320,1280]{2,1,0:T(8,128)(2,1)S(1)}, bf16[2,320,1280]{2,1,0:T(8,128)(2,1)}) custom-call(bf16[128,1280]{1,0:T(8,128)(2,1)S(1)} %shard_map.119.refs_0_, bf16[128,1280]{1,0:T(8,128)(2,1)S(1)} %collective-permute-done.3.refs_1_, bf16[128,1280]{1,0:T(8,128)(2,1)S(1)} %collective-permute-done.4.refs_2_, ...), custom_call_target="tpu_custom_call" | custom-call | tf_op jit(solution)/shard_map/pallas_call | solution.py:241
  97.7 3.6 %shard_map.123 = (bf16[512,640]{1,0:T(8,128)(2,1)S(1)}, f32[512,640]{1,0:T(8,128)S(1)}, bf16[2,128,1280]{2,1,0:T(8,128)(2,1)S(1)}, bf16[2,128,1280]{2,1,0:T(8,128)(2,1)S(1)}) custom-call(bf16[128,1280]{1,0:T(8,128)(2,1)S(1)} %shard_map.122.refs_0_, bf16[128,1280]{1,0:T(8,128)(2,1)S(1)} %collective-permute-done.13.refs_1_, ...), custom_call_target="tpu_custom_call" | custom-call | tf_op jit(solution)/shard_map/pallas_call | solution.py:241
  101.3 3.1 %collective-permute-done.33.refs_3_.refs_7_ = bf16[128,1280]{1,0:T(8,128)(2,1)S(1)} collective-permute-done((bf16[128,1280]{1,0:T(8,128)(2,1)S(1)}, bf16[128,1280]{1,0:T(8,128)(2,1)S(1)}, u32[]{:S(2)}, u32[]{:S(2)}) %collective-permute-start.33) | collective-permute-done | bytes 327712 | tf_op jit(solution)/shard_map/ppermute | solution.py:266
  104.3 3.5 %shard_map.132 = (bf16[512,640]{1,0:T(8,128)(2,1)S(1)}, bf16[2,64,1280]{2,1,0:T(8,128)(2,1)S(1)}, bf16[2,64,1280]{2,1,0:T(8,128)(2,1)S(1)}, bf16[2,64,1280]{2,1,0:T(8,128)(2,1)S(1)}, bf16[2,64,1280]{2,1,0:T(8,128)(2,1)S(1)}) custom-call(bf16[128,1280]{1,0:T(8,128)(2,1)S(1)} %get-tuple-element.91.refs_0_.refs_4_, ...), custom_call_target="tpu_custom_call" | custom-call | tf_op jit(solution)/shard_map/pallas_call | solution.py:241
  107.8 2.1 %shard_map.138 = (bf16[2,320,1280]{2,1,0:T(8,128)(2,1)S(1)}, bf16[2,320,1280]{2,1,0:T(8,128)(2,1)S(1)}) custom-call(bf16[128,1280]{1,0:T(8,128)(2,1)S(1)} %shard_map.122.refs_0_, bf16[128,1280]{1,0:T(8,128)(2,1)S(1)} %collective-permute-done.13.refs_1_, bf16[128,1280]{1,0:T(8,128)(2,1)S(1)} %collective-permute-done.14.refs_2_, ...), custom_call_target="tpu_custom_call" | custom-call | tf_op jit(solution)/shard_map/pallas_call | solution.py:241
  110.0 1.6 collective-permute-start.34
  111.6 1.5 collective-permute-start.36
  113.6 7.0 %collective-permute-done.34.refs_1_ = bf16[2,64,1280]{2,1,0:T(8,128)(2,1)S(1)} collective-permute-done((bf16[2,64,1280]{2,1,0:T(8,128)(2,1)S(1)}, bf16[2,64,1280]{2,1,0:T(8,128)(2,1)S(1)}, u32[]{:S(2)}, u32[]{:S(2)}) %collective-permute-start.34) | collective-permute-done | bytes 327712 | tf_op jit(solution)/shard_map/ppermute | solution.py:266
  120.6 1.5 collective-permute-start.16
  122.9 16.9 %collective-permute-done.28.refs_2_ = bf16[1,64,1280]{2,1,0:T(8,128)(2,1)S(1)} collective-permute-done((bf16[1,64,1280]{2,1,0:T(8,128)(2,1)S(1)}, bf16[1,64,1280]{2,1,0:T(8,128)(2,1)S(1)}, u32[]{:S(2)}, u32[]{:S(2)}) %collective-permute-start.28) | collective-permute-done | bytes 163872 | tf_op jit(solution)/shard_map/ppermute | solution.py:266
  139.8 1.5 collective-permute-start.30
  141.4 3.8 %collective-permute-done.30.refs_5_ = bf16[1,64,1280]{2,1,0:T(8,128)(2,1)S(1)} collective-permute-done((bf16[1,64,1280]{2,1,0:T(8,128)(2,1)S(1)}, bf16[1,64,1280]{2,1,0:T(8,128)(2,1)S(1)}, u32[]{:S(2)}, u32[]{:S(2)}) %collective-permute-start.30) | collective-permute-done | bytes 163872 | tf_op jit(solution)/shard_map/ppermute | solution.py:266
  145.2 1.6 collective-permute-start.35
  146.8 1.5 collective-permute-start.37
  149.0 3.2 %collective-permute-done.35.refs_2_ = bf16[1,64,1280]{2,1,0:T(8,128)(2,1)S(1)} collective-permute-done((bf16[1,64,1280]{2,1,0:T(8,128)(2,1)S(1)}, bf16[1,64,1280]{2,1,0:T(8,128)(2,1)S(1)}, u32[]{:S(2)}, u32[]{:S(2)}) %collective-permute-start.35) | collective-permute-done | bytes 163872 | tf_op jit(solution)/shard_map/ppermute | solution.py:266
  154.0 4.3 %collective-permute-done.38.refs_2_ = bf16[32,1280]{1,0:T(8,128)(2,1)S(1)} collective-permute-done((bf16[32,1280]{1,0:T(8,128)(2,1)S(1)}, bf16[32,1280]{1,0:T(8,128)(2,1)S(1)}, u32[]{:S(2)}, u32[]{:S(2)}) %collective-permute-start.38) | collective-permute-done | bytes 81952 | tf_op jit(solution)/shard_map/ppermute | solution.py:272
  158.4 4.4 %collective-permute-done.39.refs_3_ = bf16[32,1280]{1,0:T(8,128)(2,1)S(1)} collective-permute-done((bf16[32,1280]{1,0:T(8,128)(2,1)S(1)}, bf16[32,1280]{1,0:T(8,128)(2,1)S(1)}, u32[]{:S(2)}, u32[]{:S(2)}) %collective-permute-start.39) | collective-permute-done | bytes 81952 | tf_op jit(solution)/shard_map/ppermute | solution.py:272
  164.1 5.5 %collective-permute-done.40.refs_4_ = bf16[32,1280]{1,0:T(8,128)(2,1)S(1)} collective-permute-done((bf16[32,1280]{1,0:T(8,128)(2,1)S(1)}, bf16[32,1280]{1,0:T(8,128)(2,1)S(1)}, u32[]{:S(2)}, u32[]{:S(2)}) %collective-permute-start.40) | collective-permute-done | bytes 81952 | tf_op jit(solution)/shard_map/ppermute | solution.py:272
  169.6 2.1 %collective-permute-start.42 = (bf16[32,1280]{1,0:T(8,128)(2,1)S(1)}, bf16[32,1280]{1,0:T(8,128)(2,1)S(1)}, u32[]{:S(2)}, u32[]{:S(2)}) collective-permute-start(bf16[32,1280]{1,0:T(8,128)(2,1)S(1)} %get-tuple-element.102), channel_id=1, source_target_pairs={{0,3},{1,2},{2,1},{3,0},{4,7},{5,6},{6,5},{7,4},{8,11},{9,10},{10,... | collective-permute-start | bytes 245768 | tf_op jit(solution)/shard_map/ppermute | solution.py:272
  171.7 1.7 collective-permute-start.43
  173.7 6.4 %collective-permute-done.41.refs_5_ = bf16[32,1280]{1,0:T(8,128)(2,1)S(1)} collective-permute-done((bf16[32,1280]{1,0:T(8,128)(2,1)S(1)}, bf16[32,1280]{1,0:T(8,128)(2,1)S(1)}, u32[]{:S(2)}, u32[]{:S(2)}) %collective-permute-start.41) | collective-permute-done | bytes 81952 | tf_op jit(solution)/shard_map/ppermute | solution.py:272
  180.1 1.9 collective-permute-start.19
  182.0 2.7 %collective-permute-start.20 = (bf16[64,1280]{1,0:T(8,128)(2,1)S(1)}, bf16[64,1280]{1,0:T(8,128)(2,1)S(1)}, u32[]{:S(2)}, u32[]{:S(2)}) collective-permute-start(bf16[64,1280]{1,0:T(8,128)(2,1)S(1)} %get-tuple-element.75), channel_id=1, source_target_pairs={{0,3},{1,2},{2,1},{3,0},{4,7},{5,6},{6,5},{7,4},{8,11},{9,10},{10,... | collective-permute-start | bytes 491528 | tf_op jit(solution)/shard_map/ppermute | solution.py:272
  187.1 2.8 %collective-permute-done.19.refs_2_ = bf16[64,1280]{1,0:T(8,128)(2,1)S(1)} collective-permute-done((bf16[64,1280]{1,0:T(8,128)(2,1)S(1)}, bf16[64,1280]{1,0:T(8,128)(2,1)S(1)}, u32[]{:S(2)}, u32[]{:S(2)}) %collective-permute-start.19) | collective-permute-done | bytes 163872 | tf_op jit(solution)/shard_map/ppermute | solution.py:272
  191.3 2.4 %shard_map.139 = (bf16[2,320,1280]{2,1,0:T(8,128)(2,1)}, bf16[2,320,1280]{2,1,0:T(8,128)(2,1)}) custom-call(bf16[2,320,1280]{2,1,0:T(8,128)(2,1)S(1)} %get-tuple-element.107.refs_0_, bf16[2,320,1280]{2,1,0:T(8,128)(2,1)S(1)} %get-tuple-element.110.refs_1_, bf16[2,320,1280]{2,1,0:T(8,128)(2,1)S(1)} %collective-permute-done.44.refs_2_, ...), custom_call_target="tpu_custom_call" | custom-call | tf_op jit(solution)/shard_map/pallas_call | solution.py:241
  (88 shorter events, 24.9 us)
Async XLA Ops:
  0.6 82.6 %copy-start = (bf16[2,320,1280]{2,1,0:T(8,128)(2,1)S(1)}, bf16[2,320,1280]{2,1,0:T(8,128)(2,1)}, u32[]{:S(2)}) copy-start(bf16[2,320,1280]{2,1,0:T(8,128)(2,1)} %refs_4_.9) | copy-start | bytes 4915204
  0.6 80.5 %collective-permute-start.6 = (bf16[2,320,1280]{2,1,0:T(8,128)(2,1)}, bf16[2,320,1280]{2,1,0:T(8,128)(2,1)S(1)}, u32[]{:S(2)}, u32[]{:S(2)}) collective-permute-start(bf16[2,320,1280]{2,1,0:T(8,128)(2,1)} %refs_4_.9), channel_id=1, source_target_pairs={{0,4},{4,0},{8,12},{12,8},{16,20},{20,16},{24,28},{28,24},{1,5},{5... | collective-permute-start | bytes 4915208 | tf_op jit(solution)/shard_map/ppermute | solution.py:266
  1.2 80.5 %collective-permute-start.7 = (bf16[2,320,1280]{2,1,0:T(8,128)(2,1)}, bf16[2,320,1280]{2,1,0:T(8,128)(2,1)}, u32[]{:S(2)}, u32[]{:S(2)}) collective-permute-start(bf16[2,320,1280]{2,1,0:T(8,128)(2,1)} %refs_6_.7), channel_id=1, source_target_pairs={{0,4},{4,0},{8,12},{12,8},{16,20},{20,16},{24,28},{28,24},{1,5},{5... | collective-permute-start | bytes 4915208 | tf_op jit(solution)/shard_map/ppermute | solution.py:266
  7.5 5.7 %collective-permute-start = (bf16[32,1280]{1,0:T(8,128)(2,1)S(1)}, bf16[32,1280]{1,0:T(8,128)(2,1)S(1)}, u32[]{:S(2)}, u32[]{:S(2)}) collective-permute-start(bf16[32,1280]{1,0:T(8,128)(2,1)S(1)} %get-tuple-element.61), channel_id=1, source_target_pairs={{0,1},{1,0},{2,3},{3,2},{4,5},{5,4},{6,7},{7,6},{8,9},{9,8},{10,11... | collective-permute-start | bytes 245768 | tf_op jit(solution)/shard_map/ppermute | solution.py:272
  10.6 9.8 %collective-permute-start.1 = (bf16[32,1280]{1,0:T(8,128)(2,1)S(1)}, bf16[32,1280]{1,0:T(8,128)(2,1)S(1)}, u32[]{:S(2)}, u32[]{:S(2)}) collective-permute-start(bf16[32,1280]{1,0:T(8,128)(2,1)S(1)} %get-tuple-element.62), channel_id=1, source_target_pairs={{0,2},{1,3},{2,0},{3,1},{4,6},{5,7},{6,4},{7,5},{8,10},{9,11},{10,... | collective-permute-start | bytes 245768 | tf_op jit(solution)/shard_map/ppermute | solution.py:272
  13.2 7.2 %collective-permute-start.2 = (bf16[32,1280]{1,0:T(8,128)(2,1)S(1)}, bf16[32,1280]{1,0:T(8,128)(2,1)S(1)}, u32[]{:S(2)}, u32[]{:S(2)}) collective-permute-start(bf16[32,1280]{1,0:T(8,128)(2,1)S(1)} %get-tuple-element.63), channel_id=1, source_target_pairs={{0,3},{1,2},{2,1},{3,0},{4,7},{5,6},{6,5},{7,4},{8,11},{9,10},{10,... | collective-permute-start | bytes 245768 | tf_op jit(solution)/shard_map/ppermute | solution.py:272
  13.2 10.9 %collective-permute-start.10 = (bf16[32,1280]{1,0:T(8,128)(2,1)S(1)}, bf16[32,1280]{1,0:T(8,128)(2,1)S(1)}, u32[]{:S(2)}, u32[]{:S(2)}) collective-permute-start(bf16[32,1280]{1,0:T(8,128)(2,1)S(1)} %get-tuple-element.67), channel_id=1, source_target_pairs={{0,1},{1,0},{2,3},{3,2},{4,5},{5,4},{6,7},{7,6},{8,9},{9,8},{10,11... | collective-permute-start | bytes 245768 | tf_op jit(solution)/shard_map/ppermute | solution.py:272
  20.4 5.9 %collective-permute-start.11 = (bf16[32,1280]{1,0:T(8,128)(2,1)S(1)}, bf16[32,1280]{1,0:T(8,128)(2,1)S(1)}, u32[]{:S(2)}, u32[]{:S(2)}) collective-permute-start(bf16[32,1280]{1,0:T(8,128)(2,1)S(1)} %get-tuple-element.68), channel_id=1, source_target_pairs={{0,2},{1,3},{2,0},{3,1},{4,6},{5,7},{6,4},{7,5},{8,10},{9,11},{10,... | collective-permute-start | bytes 245768 | tf_op jit(solution)/shard_map/ppermute | solution.py:272
  20.4 10.4 %collective-permute-start.21 = (bf16[64,1280]{1,0:T(8,128)(2,1)S(1)}, bf16[64,1280]{1,0:T(8,128)(2,1)S(1)}, u32[]{:S(2)}, u32[]{:S(2)}) collective-permute-start(bf16[64,1280]{1,0:T(8,128)(2,1)S(1)} %get-tuple-element.81), channel_id=1, source_target_pairs={{0,1},{1,0},{2,3},{3,2},{4,5},{5,4},{6,7},{7,6},{8,9},{9,8},{10,11... | collective-permute-start | bytes 491528 | tf_op jit(solution)/shard_map/ppermute | solution.py:272
  24.2 6.6 %collective-permute-start.12 = (bf16[32,1280]{1,0:T(8,128)(2,1)S(1)}, bf16[32,1280]{1,0:T(8,128)(2,1)S(1)}, u32[]{:S(2)}, u32[]{:S(2)}) collective-permute-start(bf16[32,1280]{1,0:T(8,128)(2,1)S(1)} %get-tuple-element.69), channel_id=1, source_target_pairs={{0,3},{1,2},{2,1},{3,0},{4,7},{5,6},{6,5},{7,4},{8,11},{9,10},{10,... | collective-permute-start | bytes 245768 | tf_op jit(solution)/shard_map/ppermute | solution.py:272
  26.3 16.9 %collective-permute-start.3 = (bf16[128,1280]{1,0:T(8,128)(2,1)S(1)}, bf16[128,1280]{1,0:T(8,128)(2,1)S(1)}, u32[]{:S(2)}, u32[]{:S(2)}) collective-permute-start(bf16[128,1280]{1,0:T(8,128)(2,1)S(1)} %shard_map.119.refs_0_), channel_id=1, source_target_pairs={{0,8},{4,12},{8,0},{12,4},{16,24},{20,28},{24,16},{28,20},{1,9},{5... | collective-permute-start | bytes 983048 | tf_op jit(solution)/shard_map/ppermute | solution.py:266
  30.7 10.3 %collective-permute-start.22 = (bf16[64,1280]{1,0:T(8,128)(2,1)S(1)}, bf16[64,1280]{1,0:T(8,128)(2,1)S(1)}, u32[]{:S(2)}, u32[]{:S(2)}) collective-permute-start(bf16[64,1280]{1,0:T(8,128)(2,1)S(1)} %get-tuple-element.82), channel_id=1, source_target_pairs={{0,2},{1,3},{2,0},{3,1},{4,6},{5,7},{6,4},{7,5},{8,10},{9,11},{10,... | collective-permute-start | bytes 491528 | tf_op jit(solution)/shard_map/ppermute | solution.py:272
  30.7 11.8 %collective-permute-start.23 = (bf16[64,1280]{1,0:T(8,128)(2,1)S(1)}, bf16[64,1280]{1,0:T(8,128)(2,1)S(1)}, u32[]{:S(2)}, u32[]{:S(2)}) collective-permute-start(bf16[64,1280]{1,0:T(8,128)(2,1)S(1)} %get-tuple-element.83), channel_id=1, source_target_pairs={{0,3},{1,2},{2,1},{3,0},{4,7},{5,6},{6,5},{7,4},{8,11},{9,10},{10,... | collective-permute-start | bytes 491528 | tf_op jit(solution)/shard_map/ppermute | solution.py:272
  41.0 10.6 %collective-permute-start.4 = (bf16[128,1280]{1,0:T(8,128)(2,1)S(1)}, bf16[128,1280]{1,0:T(8,128)(2,1)S(1)}, u32[]{:S(2)}, u32[]{:S(2)}) collective-permute-start(bf16[128,1280]{1,0:T(8,128)(2,1)S(1)} %shard_map.119.refs_0_), channel_id=1, source_target_pairs={{0,16},{4,20},{8,24},{12,28},{16,0},{20,4},{24,8},{28,12},{1,17},{... | collective-permute-start | bytes 983048 | tf_op jit(solution)/shard_map/ppermute | solution.py:266
  42.6 16.0 %collective-permute-start.14 = (bf16[128,1280]{1,0:T(8,128)(2,1)S(1)}, bf16[128,1280]{1,0:T(8,128)(2,1)S(1)}, u32[]{:S(2)}, u32[]{:S(2)}) collective-permute-start(bf16[128,1280]{1,0:T(8,128)(2,1)S(1)} %shard_map.122.refs_0_), channel_id=1, source_target_pairs={{0,16},{4,20},{8,24},{12,28},{16,0},{20,4},{24,8},{28,12},{1,17},{... | collective-permute-start | bytes 983048 | tf_op jit(solution)/shard_map/ppermute | solution.py:266
  43.2 16.9 %collective-permute-start.24 = (bf16[128,1280]{1,0:T(8,128)(2,1)S(1)}, bf16[128,1280]{1,0:T(8,128)(2,1)S(1)}, u32[]{:S(2)}, u32[]{:S(2)}) collective-permute-start(bf16[128,1280]{1,0:T(8,128)(2,1)S(1)} %get-tuple-element.84.refs_0_.refs_4_), channel_id=1, source_target_pairs={{0,8},{4,12},{8,0},{12,4},{16,24},{20,28},{24,16},{28,20},{1,9},{5... | collective-permute-start | bytes 983048 | tf_op jit(solution)/shard_map/ppermute | solution.py:266
  51.6 14.0 %collective-permute-start.25 = (bf16[128,1280]{1,0:T(8,128)(2,1)S(1)}, bf16[128,1280]{1,0:T(8,128)(2,1)S(1)}, u32[]{:S(2)}, u32[]{:S(2)}) collective-permute-start(bf16[128,1280]{1,0:T(8,128)(2,1)S(1)} %get-tuple-element.84.refs_0_.refs_4_), channel_id=1, source_target_pairs={{0,16},{4,20},{8,24},{12,28},{16,0},{20,4},{24,8},{28,12},{1,17},{... | collective-permute-start | bytes 983048 | tf_op jit(solution)/shard_map/ppermute | solution.py:266
  58.6 14.0 %collective-permute-start.32 = (bf16[128,1280]{1,0:T(8,128)(2,1)S(1)}, bf16[128,1280]{1,0:T(8,128)(2,1)S(1)}, u32[]{:S(2)}, u32[]{:S(2)}) collective-permute-start(bf16[128,1280]{1,0:T(8,128)(2,1)S(1)} %get-tuple-element.91.refs_0_.refs_4_), channel_id=1, source_target_pairs={{0,16},{4,20},{8,24},{12,28},{16,0},{20,4},{24,8},{28,12},{1,17},{... | collective-permute-start | bytes 983048 | tf_op jit(solution)/shard_map/ppermute | solution.py:266
  60.1 19.5 %collective-permute-start.5 = (bf16[128,1280]{1,0:T(8,128)(2,1)S(1)}, bf16[128,1280]{1,0:T(8,128)(2,1)S(1)}, u32[]{:S(2)}, u32[]{:S(2)}) collective-permute-start(bf16[128,1280]{1,0:T(8,128)(2,1)S(1)} %collective-permute-done.3.refs_1_), channel_id=1, source_target_pairs={{0,16},{4,20},{8,24},{12,28},{16,0},{20,4},{24,8},{28,12},{1,17},{... | collective-permute-start | bytes 983048 | tf_op jit(solution)/shard_map/ppermute | solution.py:266
  65.6 22.7 %collective-permute-start.26 = (bf16[128,1280]{1,0:T(8,128)(2,1)S(1)}, bf16[128,1280]{1,0:T(8,128)(2,1)S(1)}, u32[]{:S(2)}, u32[]{:S(2)}) collective-permute-start(bf16[128,1280]{1,0:T(8,128)(2,1)S(1)} %collective-permute-done.24.refs_1_.refs_5_), channel_id=1, source_target_pairs={{0,16},{4,20},{8,24},{12,28},{16,0},{20,4},{24,8},{28,12},{1,17},{... | collective-permute-start | bytes 983048 | tf_op jit(solution)/shard_map/ppermute | solution.py:266
  72.7 20.4 %collective-permute-start.13 = (bf16[128,1280]{1,0:T(8,128)(2,1)S(1)}, bf16[128,1280]{1,0:T(8,128)(2,1)S(1)}, u32[]{:S(2)}, u32[]{:S(2)}) collective-permute-start(bf16[128,1280]{1,0:T(8,128)(2,1)S(1)} %shard_map.122.refs_0_), channel_id=1, source_target_pairs={{0,8},{4,12},{8,0},{12,4},{16,24},{20,28},{24,16},{28,20},{1,9},{5... | collective-permute-start | bytes 983048 | tf_op jit(solution)/shard_map/ppermute | solution.py:266
  79.7 18.0 %collective-permute-start.15 = (bf16[128,1280]{1,0:T(8,128)(2,1)S(1)}, bf16[128,1280]{1,0:T(8,128)(2,1)S(1)}, u32[]{:S(2)}, u32[]{:S(2)}) collective-permute-start(bf16[128,1280]{1,0:T(8,128)(2,1)S(1)} %collective-permute-done.14.refs_2_), channel_id=1, source_target_pairs={{0,8},{4,12},{8,0},{12,4},{16,24},{20,28},{24,16},{28,20},{1,9},{5... | collective-permute-start | bytes 983048 | tf_op jit(solution)/shard_map/ppermute | solution.py:266
  81.2 20.1 %collective-permute-start.31 = (bf16[128,1280]{1,0:T(8,128)(2,1)S(1)}, bf16[128,1280]{1,0:T(8,128)(2,1)S(1)}, u32[]{:S(2)}, u32[]{:S(2)}) collective-permute-start(bf16[128,1280]{1,0:T(8,128)(2,1)S(1)} %get-tuple-element.91.refs_0_.refs_4_), channel_id=1, source_target_pairs={{0,8},{4,12},{8,0},{12,4},{16,24},{20,28},{24,16},{28,20},{1,9},{5... | collective-permute-start | bytes 983048 | tf_op jit(solution)/shard_map/ppermute | solution.py:266
  81.7 22.6 %collective-permute-start.33 = (bf16[128,1280]{1,0:T(8,128)(2,1)S(1)}, bf16[128,1280]{1,0:T(8,128)(2,1)S(1)}, u32[]{:S(2)}, u32[]{:S(2)}) collective-permute-start(bf16[128,1280]{1,0:T(8,128)(2,1)S(1)} %collective-permute-done.32.refs_2_.refs_6_), channel_id=1, source_target_pairs={{0,8},{4,12},{8,0},{12,4},{16,24},{20,28},{24,16},{28,20},{1,9},{5... | collective-permute-start | bytes 983048 | tf_op jit(solution)/shard_map/ppermute | solution.py:266
  92.6 19.0 %collective-permute-start.27 = (bf16[2,64,1280]{2,1,0:T(8,128)(2,1)}, bf16[2,64,1280]{2,1,0:T(8,128)(2,1)S(1)}, u32[]{:S(2)}, u32[]{:S(2)}) collective-permute-start(bf16[2,64,1280]{2,1,0:T(8,128)(2,1)} %get-tuple-element.87), channel_id=1, source_target_pairs={{0,8},{4,12},{8,0},{12,4},{16,24},{20,28},{24,16},{28,20},{1,9},{5... | collective-permute-start | bytes 983048 | tf_op jit(solution)/shard_map/ppermute | solution.py:266
  93.1 20.0 %collective-permute-start.29 = (bf16[2,64,1280]{2,1,0:T(8,128)(2,1)S(1)}, bf16[2,64,1280]{2,1,0:T(8,128)(2,1)S(1)}, u32[]{:S(2)}, u32[]{:S(2)}) collective-permute-start(bf16[2,64,1280]{2,1,0:T(8,128)(2,1)S(1)} %get-tuple-element.89), channel_id=1, source_target_pairs={{0,16},{4,20},{8,24},{12,28},{16,0},{20,4},{24,8},{28,12},{1,17},{... | collective-permute-start | bytes 983048 | tf_op jit(solution)/shard_map/ppermute | solution.py:266
  97.7 93.6 %collective-permute-start.44 = (bf16[2,320,1280]{2,1,0:T(8,128)(2,1)}, bf16[2,320,1280]{2,1,0:T(8,128)(2,1)S(1)}, u32[]{:S(2)}, u32[]{:S(2)}) collective-permute-start(bf16[2,320,1280]{2,1,0:T(8,128)(2,1)} %get-tuple-element.111), channel_id=1, source_target_pairs={{0,4},{4,0},{8,12},{12,8},{16,20},{20,16},{24,28},{28,24},{1,5},{5... | collective-permute-start | bytes 4915208 | tf_op jit(solution)/shard_map/ppermute | solution.py:266
  109.9 81.4 %collective-permute-start.45 = (bf16[2,320,1280]{2,1,0:T(8,128)(2,1)S(1)}, bf16[2,320,1280]{2,1,0:T(8,128)(2,1)S(1)}, u32[]{:S(2)}, u32[]{:S(2)}) collective-permute-start(bf16[2,320,1280]{2,1,0:T(8,128)(2,1)S(1)} %get-tuple-element.112), channel_id=1, source_target_pairs={{0,4},{4,0},{8,12},{12,8},{16,20},{20,16},{24,28},{28,24},{1,5},{5... | collective-permute-start | bytes 4915208 | tf_op jit(solution)/shard_map/ppermute | solution.py:266
  110.0 10.7 %collective-permute-start.34 = (bf16[2,64,1280]{2,1,0:T(8,128)(2,1)S(1)}, bf16[2,64,1280]{2,1,0:T(8,128)(2,1)S(1)}, u32[]{:S(2)}, u32[]{:S(2)}) collective-permute-start(bf16[2,64,1280]{2,1,0:T(8,128)(2,1)S(1)} %get-tuple-element.94), channel_id=1, source_target_pairs={{0,8},{4,12},{8,0},{12,4},{16,24},{20,28},{24,16},{28,20},{1,9},{5... | collective-permute-start | bytes 983048 | tf_op jit(solution)/shard_map/ppermute | solution.py:266
  111.6 10.7 %collective-permute-start.36 = (bf16[2,64,1280]{2,1,0:T(8,128)(2,1)S(1)}, bf16[2,64,1280]{2,1,0:T(8,128)(2,1)S(1)}, u32[]{:S(2)}, u32[]{:S(2)}) collective-permute-start(bf16[2,64,1280]{2,1,0:T(8,128)(2,1)S(1)} %get-tuple-element.96), channel_id=1, source_target_pairs={{0,16},{4,20},{8,24},{12,28},{16,0},{20,4},{24,8},{28,12},{1,17},{... | collective-permute-start | bytes 983048 | tf_op jit(solution)/shard_map/ppermute | solution.py:266
  113.1 33.7 %collective-permute-start.8 = (bf16[2,128,1280]{2,1,0:T(8,128)(2,1)S(1)}, bf16[2,128,1280]{2,1,0:T(8,128)(2,1)S(1)}, u32[]{:S(2)}, u32[]{:S(2)}) collective-permute-start(bf16[2,128,1280]{2,1,0:T(8,128)(2,1)S(1)} %get-tuple-element.65), channel_id=1, source_target_pairs={{0,8},{4,12},{8,0},{12,4},{16,24},{20,28},{24,16},{28,20},{1,9},{5... | collective-permute-start | bytes 1966088 | tf_op jit(solution)/shard_map/ppermute | solution.py:266
  120.6 27.8 %collective-permute-start.16 = (bf16[2,128,1280]{2,1,0:T(8,128)(2,1)S(1)}, bf16[2,128,1280]{2,1,0:T(8,128)(2,1)S(1)}, u32[]{:S(2)}, u32[]{:S(2)}) collective-permute-start(bf16[2,128,1280]{2,1,0:T(8,128)(2,1)S(1)} %get-tuple-element.71), channel_id=1, source_target_pairs={{0,16},{4,20},{8,24},{12,28},{16,0},{20,4},{24,8},{28,12},{1,17},{... | collective-permute-start | bytes 1966088 | tf_op jit(solution)/shard_map/ppermute | solution.py:266
  122.2 17.6 %collective-permute-start.28 = (bf16[1,64,1280]{2,1,0:T(8,128)(2,1)S(1)}, bf16[1,64,1280]{2,1,0:T(8,128)(2,1)S(1)}, u32[]{:S(2)}, u32[]{:S(2)}) collective-permute-start(bf16[1,64,1280]{2,1,0:T(8,128)(2,1)S(1)} %shard_map.129), channel_id=1, source_target_pairs={{0,16},{4,20},{8,24},{12,28},{16,0},{20,4},{24,8},{28,12},{1,17},{... | collective-permute-start | bytes 491528 | tf_op jit(solution)/shard_map/ppermute | solution.py:266
  139.8 5.3 %collective-permute-start.30 = (bf16[1,64,1280]{2,1,0:T(8,128)(2,1)S(1)}, bf16[1,64,1280]{2,1,0:T(8,128)(2,1)S(1)}, u32[]{:S(2)}, u32[]{:S(2)}) collective-permute-start(bf16[1,64,1280]{2,1,0:T(8,128)(2,1)S(1)} %shard_map.130), channel_id=1, source_target_pairs={{0,8},{4,12},{8,0},{12,4},{16,24},{20,28},{24,16},{28,20},{1,9},{5... | collective-permute-start | bytes 491528 | tf_op jit(solution)/shard_map/ppermute | solution.py:266
  145.2 7.1 %collective-permute-start.35 = (bf16[1,64,1280]{2,1,0:T(8,128)(2,1)S(1)}, bf16[1,64,1280]{2,1,0:T(8,128)(2,1)S(1)}, u32[]{:S(2)}, u32[]{:S(2)}) collective-permute-start(bf16[1,64,1280]{2,1,0:T(8,128)(2,1)S(1)} %shard_map.133), channel_id=1, source_target_pairs={{0,16},{4,20},{8,24},{12,28},{16,0},{20,4},{24,8},{28,12},{1,17},{... | collective-permute-start | bytes 491528 | tf_op jit(solution)/shard_map/ppermute | solution.py:266
  146.8 7.1 %collective-permute-start.37 = (bf16[1,64,1280]{2,1,0:T(8,128)(2,1)S(1)}, bf16[1,64,1280]{2,1,0:T(8,128)(2,1)S(1)}, u32[]{:S(2)}, u32[]{:S(2)}) collective-permute-start(bf16[1,64,1280]{2,1,0:T(8,128)(2,1)S(1)} %shard_map.134), channel_id=1, source_target_pairs={{0,8},{4,12},{8,0},{12,4},{16,24},{20,28},{24,16},{28,20},{1,9},{5... | collective-permute-start | bytes 491528 | tf_op jit(solution)/shard_map/ppermute | solution.py:266
  148.4 21.2 %collective-permute-start.9 = (bf16[1,128,1280]{2,1,0:T(8,128)(2,1)S(1)}, bf16[1,128,1280]{2,1,0:T(8,128)(2,1)S(1)}, u32[]{:S(2)}, u32[]{:S(2)}) collective-permute-start(bf16[1,128,1280]{2,1,0:T(8,128)(2,1)S(1)} %shard_map.121), channel_id=1, source_target_pairs={{0,16},{4,20},{8,24},{12,28},{16,0},{20,4},{24,8},{28,12},{1,17},{... | collective-permute-start | bytes 983048 | tf_op jit(solution)/shard_map/ppermute | solution.py:266
  152.2 19.5 %collective-permute-start.17 = (bf16[1,128,1280]{2,1,0:T(8,128)(2,1)S(1)}, bf16[1,128,1280]{2,1,0:T(8,128)(2,1)S(1)}, u32[]{:S(2)}, u32[]{:S(2)}) collective-permute-start(bf16[1,128,1280]{2,1,0:T(8,128)(2,1)S(1)} %shard_map.124), channel_id=1, source_target_pairs={{0,8},{4,12},{8,0},{12,4},{16,24},{20,28},{24,16},{28,20},{1,9},{5... | collective-permute-start | bytes 983048 | tf_op jit(solution)/shard_map/ppermute | solution.py:266
  153.9 4.4 %collective-permute-start.38 = (bf16[32,1280]{1,0:T(8,128)(2,1)S(1)}, bf16[32,1280]{1,0:T(8,128)(2,1)S(1)}, u32[]{:S(2)}, u32[]{:S(2)}) collective-permute-start(bf16[32,1280]{1,0:T(8,128)(2,1)S(1)} %get-tuple-element.98), channel_id=1, source_target_pairs={{0,1},{1,0},{2,3},{3,2},{4,5},{5,4},{6,7},{7,6},{8,9},{9,8},{10,11... | collective-permute-start | bytes 245768 | tf_op jit(solution)/shard_map/ppermute | solution.py:272
  158.4 4.4 %collective-permute-start.39 = (bf16[32,1280]{1,0:T(8,128)(2,1)S(1)}, bf16[32,1280]{1,0:T(8,128)(2,1)S(1)}, u32[]{:S(2)}, u32[]{:S(2)}) collective-permute-start(bf16[32,1280]{1,0:T(8,128)(2,1)S(1)} %get-tuple-element.99), channel_id=1, source_target_pairs={{0,1},{1,0},{2,3},{3,2},{4,5},{5,4},{6,7},{7,6},{8,9},{9,8},{10,11... | collective-permute-start | bytes 245768 | tf_op jit(solution)/shard_map/ppermute | solution.py:272
  162.8 6.8 %collective-permute-start.40 = (bf16[32,1280]{1,0:T(8,128)(2,1)S(1)}, bf16[32,1280]{1,0:T(8,128)(2,1)S(1)}, u32[]{:S(2)}, u32[]{:S(2)}) collective-permute-start(bf16[32,1280]{1,0:T(8,128)(2,1)S(1)} %get-tuple-element.100), channel_id=1, source_target_pairs={{0,2},{1,3},{2,0},{3,1},{4,6},{5,7},{6,4},{7,5},{8,10},{9,11},{10,... | collective-permute-start | bytes 245768 | tf_op jit(solution)/shard_map/ppermute | solution.py:272
  169.6 10.5 %collective-permute-start.41 = (bf16[32,1280]{1,0:T(8,128)(2,1)S(1)}, bf16[32,1280]{1,0:T(8,128)(2,1)S(1)}, u32[]{:S(2)}, u32[]{:S(2)}) collective-permute-start(bf16[32,1280]{1,0:T(8,128)(2,1)S(1)} %get-tuple-element.101), channel_id=1, source_target_pairs={{0,2},{1,3},{2,0},{3,1},{4,6},{5,7},{6,4},{7,5},{8,10},{9,11},{10,... | collective-permute-start | bytes 245768 | tf_op jit(solution)/shard_map/ppermute | solution.py:272
  169.6 10.5 %collective-permute-start.42 = (bf16[32,1280]{1,0:T(8,128)(2,1)S(1)}, bf16[32,1280]{1,0:T(8,128)(2,1)S(1)}, u32[]{:S(2)}, u32[]{:S(2)}) collective-permute-start(bf16[32,1280]{1,0:T(8,128)(2,1)S(1)} %get-tuple-element.102), channel_id=1, source_target_pairs={{0,3},{1,2},{2,1},{3,0},{4,7},{5,6},{6,5},{7,4},{8,11},{9,10},{10,... | collective-permute-start | bytes 245768 | tf_op jit(solution)/shard_map/ppermute | solution.py:272
  171.7 12.9 %copy-start.6 = (bf16[128,1280]{1,0:T(8,128)(2,1)S(1)}, bf16[128,1280]{1,0:T(8,128)(2,1)}, u32[]{:S(2)}) copy-start(bf16[128,1280]{1,0:T(8,128)(2,1)} %refs_9_.1) | copy-start | bytes 983044
  171.7 10.2 %collective-permute-start.43 = (bf16[32,1280]{1,0:T(8,128)(2,1)S(1)}, bf16[32,1280]{1,0:T(8,128)(2,1)S(1)}, u32[]{:S(2)}, u32[]{:S(2)}) collective-permute-start(bf16[32,1280]{1,0:T(8,128)(2,1)S(1)} %get-tuple-element.103), channel_id=1, source_target_pairs={{0,3},{1,2},{2,1},{3,0},{4,7},{5,6},{6,5},{7,4},{8,11},{9,10},{10,... | collective-permute-start | bytes 245768 | tf_op jit(solution)/shard_map/ppermute | solution.py:272
  180.1 7.0 %collective-permute-start.18 = (bf16[64,1280]{1,0:T(8,128)(2,1)S(1)}, bf16[64,1280]{1,0:T(8,128)(2,1)S(1)}, u32[]{:S(2)}, u32[]{:S(2)}) collective-permute-start(bf16[64,1280]{1,0:T(8,128)(2,1)S(1)} %get-tuple-element.73), channel_id=1, source_target_pairs={{0,1},{1,0},{2,3},{3,2},{4,5},{5,4},{6,7},{7,6},{8,9},{9,8},{10,11... | collective-permute-start | bytes 491528 | tf_op jit(solution)/shard_map/ppermute | solution.py:272
  180.1 9.8 %collective-permute-start.19 = (bf16[64,1280]{1,0:T(8,128)(2,1)S(1)}, bf16[64,1280]{1,0:T(8,128)(2,1)S(1)}, u32[]{:S(2)}, u32[]{:S(2)}) collective-permute-start(bf16[64,1280]{1,0:T(8,128)(2,1)S(1)} %get-tuple-element.74), channel_id=1, source_target_pairs={{0,2},{1,3},{2,0},{3,1},{4,6},{5,7},{6,4},{7,5},{8,10},{9,11},{10,... | collective-permute-start | bytes 491528 | tf_op jit(solution)/shard_map/ppermute | solution.py:272
  182.0 7.9 %collective-permute-start.20 = (bf16[64,1280]{1,0:T(8,128)(2,1)S(1)}, bf16[64,1280]{1,0:T(8,128)(2,1)S(1)}, u32[]{:S(2)}, u32[]{:S(2)}) collective-permute-start(bf16[64,1280]{1,0:T(8,128)(2,1)S(1)} %get-tuple-element.75), channel_id=1, source_target_pairs={{0,3},{1,2},{2,1},{3,0},{4,7},{5,6},{6,5},{7,4},{8,11},{9,10},{10,... | collective-permute-start | bytes 491528 | tf_op jit(solution)/shard_map/ppermute | solution.py:272
  (9 other events, 22.7 us)
where the time goes:
time: 194 us
  waiting for transfers between devices  105 us (54%)
  starting transfers between devices  53.8 us (28%)
  Pallas kernels  27.7 us (14%)
  local copies, waits for them, and re-layouts  6.06 us (3%)
    ppermute x28, waiting for transfers between devices, swap(): return lax.ppermute(values, 'dp', [(i, i ^ mask) for i in range(groups)])  62.9 us
    ppermute x18, waiting for transfers between devices, cross(): lax.ppermute(pieces[s], 'expert', [(i, i ^ s) for i in range(planes)])  42.4 us
    ppermute x28, starting transfers between devices, swap(): return lax.ppermute(values, 'dp', [(i, i ^ mask) for i in range(groups)])  30 us
    pallas_call x21, Pallas kernels, run(): pl.pallas_call(kernel, out_shape=outs, grid=(1,), in_specs=specs, out_spe...  26.1 us
    ppermute x18, starting transfers between devices, cross(): lax.ppermute(pieces[s], 'expert', [(i, i ^ s) for i in range(planes)])  23.8 us
    unnamed x22, local copies, waits for them, and re-layouts  6.06 us
  transfers between devices with their start and end apart: 46, of which 22 were waited for; matrix products, arithmetic and copies ran while one was open for 0% of the time, Pallas kernels for 13%

commit v1 on v0

--- a/solution.py
+++ b/solution.py
@@ -35,19 +35,27 @@
 
 
 def route_kernel(
-    planes, local, me_ref, tok_hbm, cot_hbm, gate_ref, ids_ref, seg_ref, keep_ref, *refs
+    planes, local, me_ref, *refs
 ):
-    outs, (tok_ref, cot_ref, sems) = refs[:-3], refs[-3:]
-    tok_copy = pltpu.make_async_copy(tok_hbm, tok_ref, sems.at[0])
-    cot_copy = pltpu.make_async_copy(cot_hbm, cot_ref, sems.at[1])
-    tok_copy.start()
-    cot_copy.start()
+    outs, sems = refs[6:-7], refs[-1]
+    copies = [
+        pltpu.make_async_copy(source, held, sems.at[index])
+        for index, (source, held) in enumerate(zip(refs[:6], refs[-7:-1]))
+    ]
+    for copy in copies:
+        copy.start()
+    gate_ref, ids_ref, seg_ref, keep_ref, tok_ref, cot_ref = refs[-7:-1]
+    *small_copies, tok_copy, cot_copy = copies
+    for copy in small_copies:
+        copy.wait()
     top, toks = ids_ref.shape
     experts = planes * local
     cap = top * toks // experts
-    feature_refs = [outs[l * planes : (l + 1) * planes] for l in range(local)]
-    grad_refs = outs[local * planes : (local + 1) * planes]
-    target_ref, weight_ref, alive_ref = outs[(local + 1) * planes :]
+    own_features_ref, own_grads_ref, *outs = outs
+    others = planes - 1
+    feature_refs = [outs[l * others : (l + 1) * others] for l in range(local)]
+    grad_refs = outs[local * others : (local + 1) * others]
+    target_ref, weight_ref, alive_ref = outs[(local + 1) * others :]
     seg = seg_ref[...]
     spot = lax.broadcasted_iota(jnp.int32, seg.shape, 1).astype(jnp.float32)
     alive_row = jnp.zeros(seg.shape, jnp.float32)
@@ -90,21 +98,23 @@
     for k in range(1, top):
         every_hot = every_hot + hots[k]
     features = dot(every_hot, low, 0, 0).astype(jnp.bfloat16)
-    for away in range(planes):
+    own_features_ref[...] = features[: local * cap]
+    for away in range(1, planes):
         base = away * local * cap
         for l in range(local):
-            feature_refs[l][away][...] = features[base + l * cap : base + (l + 1) * cap]
+            feature_refs[l][away - 1][...] = features[base + l * cap : base + (l + 1) * cap]
     cot_copy.wait()
     cot = cot_ref[...].astype(jnp.float32)
     scaled = [(cot * weight).astype(jnp.bfloat16) for weight in weights]
     grads = dot(jnp.concatenate(hots, 0), jnp.concatenate(scaled, 0), 0, 0).astype(jnp.bfloat16)
-    for away in range(planes):
+    own_grads_ref[...] = grads[: local * cap]
+    for away in range(1, planes):
         base = away * local * cap
-        grad_refs[away][...] = grads[base : base + local * cap]
-
-
-def join_kernel(planes, cap, *refs):
-    piece_refs, outs = refs[:planes], refs[planes:]
+        grad_refs[away - 1][...] = grads[base : base + local * cap]
+
+
+def join_kernel(others, cap, *refs):
+    piece_refs, outs = refs[:others], refs[others:]
     for l, out in enumerate(outs):
         for away, ref in enumerate(piece_refs):
             out[away * cap : (away + 1) * cap] = ref[l * cap : (l + 1) * cap]
@@ -117,10 +127,17 @@
     refs[-1][0] = total.astype(jnp.bfloat16)
 
 
-def forward_kernel(blocks, parts, *refs):
-    rows_refs = refs[:blocks]
-    up_own, up_pair, down_own, down_pair, hidden_ref, slope_ref = refs[blocks : blocks + 6]
-    rows = jnp.concatenate([ref[...] for ref in rows_refs], 0)
+def joined(own_refs, other_refs):
+    return jnp.concatenate(
+        [ref[...] for pair in zip(own_refs, other_refs) for ref in pair], 0
+    )
+
+
+def forward_kernel(blocks, parts, held, *refs):
+    rows = joined(refs[:blocks], refs[blocks : 2 * blocks])
+    up_own, up_pair, down_own, down_pair = refs[2 * blocks : 2 * blocks + 4]
+    held_refs = refs[2 * blocks + 4 : 2 * blocks + 4 + held]
+    hidden_ref, slope_ref, *outs = refs[2 * blocks + 4 + held :]
     up = jnp.concatenate([up_own[0], up_pair[0]], 0)
     pre = dot(rows, up, 1, 1)
     half = 0.5 * (1.0 + lax.erf(pre * root_half))
@@ -128,38 +145,41 @@
     hidden_ref[...] = hidden
     slope_ref[...] = half + pre * jnp.exp(-0.5 * pre * pre) * density_scale
     down = jnp.concatenate([down_own[0], down_pair[0]], 0)
-    spread(dot(hidden, down, 1, 0), blocks, parts, refs[blocks + 6 :])
-
-
-def spread(result, blocks, parts, refs):
+    spread(dot(hidden, down, 1, 0), blocks, parts, held_refs, outs)
+
+
+def spread(result, blocks, parts, held_refs, outs):
     block_rows = result.shape[0] // blocks
+    for held_ref, ref in zip(held_refs, outs):
+        ref[:, : held_ref.shape[1]] = held_ref[...]
     for number, (start, stop, slots) in enumerate(parts):
         for index, pair in enumerate(slots):
-            for ref, block in zip(refs[2 * number : 2 * number + 2], pair):
+            for ref, block in zip(outs[2 * number : 2 * number + 2], pair):
                 base = block * block_rows
-                ref[index] = result[base + start : base + stop].astype(jnp.bfloat16)
-
-
-def backward_kernel(blocks, parts, *refs):
-    grad_refs = refs[:blocks]
-    up_own, up_pair, down_own, down_pair, slope_ref, dpre_ref = refs[blocks : blocks + 6]
-    grads = jnp.concatenate([ref[...] for ref in grad_refs], 0)
+                end = ref.shape[1]
+                ref[index, end - (stop - start) : end] = result[
+                    base + start : base + stop
+                ].astype(jnp.bfloat16)
+
+
+def backward_kernel(blocks, parts, held, *refs):
+    grads = joined(refs[:blocks], refs[blocks : 2 * blocks])
+    up_own, up_pair, down_own, down_pair, slope_ref = refs[2 * blocks : 2 * blocks + 5]
+    held_refs = refs[2 * blocks + 5 : 2 * blocks + 5 + held]
+    dpre_ref, *outs = refs[2 * blocks + 5 + held :]
     down = jnp.concatenate([down_own[0], down_pair[0]], 0)
     dpre = (dot(grads, down, 1, 1) * slope_ref[...]).astype(jnp.bfloat16)
     dpre_ref[...] = dpre
     up = jnp.concatenate([up_own[0], up_pair[0]], 0)
-    spread(dot(dpre, up, 1, 0), blocks, parts, refs[blocks + 6 :])
+    spread(dot(dpre, up, 1, 0), blocks, parts, held_refs, outs)
 
 
 def weight_kernel(blocks, *refs):
-    rows_refs = refs[:blocks]
-    grad_refs = refs[blocks : 2 * blocks]
-    hidden_ref, dpre_ref, own_ref, pair_ref = refs[2 * blocks :]
+    rows = joined(refs[:blocks], refs[blocks : 2 * blocks])
+    grads = joined(refs[2 * blocks : 3 * blocks], refs[3 * blocks : 4 * blocks])
+    hidden_ref, dpre_ref, own_ref, pair_ref = refs[4 * blocks :]
     units = own_ref.shape[1]
-    for index, (left_ref, right_refs) in enumerate(
-        ((dpre_ref, rows_refs), (hidden_ref, grad_refs))
-    ):
-        right = jnp.concatenate([ref[...] for ref in right_refs], 0)
+    for index, (left_ref, right) in enumerate(((dpre_ref, rows), (hidden_ref, grads))):
         product = dot(left_ref[...], right, 0, 0)
         own_ref[index] = product[:units].astype(jnp.bfloat16)
         pair_ref[index] = product[units:].astype(jnp.bfloat16)
@@ -176,27 +196,32 @@
             ).astype(jnp.bfloat16)
 
 
+def summed(refs):
+    total = refs[0][0].astype(jnp.float32)
+    for ref in refs[1:]:
+        total = total + ref[0].astype(jnp.float32)
+    return total.astype(jnp.bfloat16)
+
+
 def finish_kernel(groups, *refs):
     outs = refs[sum(count for counts in groups for count in counts) :]
     cap = outs[0].shape[0] // len(groups)
     used = 0
     for l, counts in enumerate(groups):
-        away = 0
+        sums = []
         for count in counts:
-            total = refs[used][0].astype(jnp.float32)
-            for ref in refs[used + 1 : used + count]:
-                total = total + ref[0].astype(jnp.float32)
+            sums.append(summed(refs[used : used + count]))
             used += count
-            low = total.astype(jnp.bfloat16)
-            for index in range(low.shape[0] // cap):
-                outs[away][l * cap : (l + 1) * cap] = low[index * cap : (index + 1) * cap]
-                away += 1
-
-
-def output_kernel(planes, *refs):
-    result_refs = refs[:planes]
-    tok_ref, cot_ref, target_ref, weight_ref, alive_ref, out_ref, gating_ref = refs[planes:]
-    results = jnp.concatenate([ref[...] for ref in result_refs], 0)
+        low = jnp.concatenate(sums, 0)
+        for index, out in enumerate(outs):
+            out[l * cap : (l + 1) * cap] = low[index * cap : (index + 1) * cap]
+
+
+def output_kernel(count, *refs):
+    tok_ref, cot_ref, target_ref, weight_ref, alive_ref, out_ref, gating_ref = refs[-7:]
+    results = jnp.concatenate(
+        [summed(refs[:count])] + [ref[...] for ref in refs[count:-7]], 0
+    )
     toks = tok_ref.shape[0]
     row = lax.broadcasted_iota(jnp.int32, (toks, toks), 0)
     same = row == lax.broadcasted_iota(jnp.int32, (toks, toks), 1)
@@ -210,10 +235,9 @@
     out_ref[...] = total.astype(jnp.bfloat16)
 
 
-def input_kernel(planes, local, *refs):
-    grad_refs = refs[: planes * local]
-    tok_ref, cot_ref, target_ref, alive_ref, out_ref = refs[planes * local :]
-    grads = jnp.concatenate([ref[...] for ref in grad_refs], 0)
+def input_kernel(count, *refs):
+    tok_ref, cot_ref, target_ref, alive_ref, out_ref = refs[-5:]
+    grads = jnp.concatenate([summed(refs[:count])] + [ref[...] for ref in refs[count:-5]], 0)
     hot = one_hot(target_ref[:, 0:1], grads.shape[0])
     for k in range(1, target_ref.shape[1]):
         hot = hot + one_hot(target_ref[:, k : k + 1], grads.shape[0])
@@ -234,9 +258,19 @@
     return pl.BlockSpec((1,) + array.shape[1:], lambda *_: (index,) + (0,) * (rank - 1))
 
 
+def slab(array, index, rows):
+    return pl.BlockSpec((rows, array.shape[1]), lambda *_: (index, 0))
+
+
+def spec_of(item):
+    if not isinstance(item, tuple):
+        return whole(item)
+    return part(*item) if len(item) == 2 else slab(*item)
+
+
 def run(kernel, inputs, outs):
     arrays = [item[0] if isinstance(item, tuple) else item for item in inputs]
-    specs = [part(*item) if isinstance(item, tuple) else whole(item) for item in inputs]
+    specs = [spec_of(item) for item in inputs]
     outs = [jax.ShapeDtypeStruct(shape, dtype) for shape, dtype in outs]
     return pl.pallas_call(
         kernel,
@@ -267,11 +301,9 @@
 
     def cross(pieces):
         away = []
-        for s in range(1, planes):
-            away.append(
-                lax.ppermute(pieces[s], "expert", [(i, i ^ s) for i in range(planes)])
-            )
-        return [pieces[0]] + away
+        for s, piece in enumerate(pieces, 1):
+            away.append(lax.ppermute(piece, "expert", [(i, i ^ s) for i in range(planes)]))
+        return away
 
     def order_of(index):
         shift = index % len(bits)
@@ -310,76 +342,93 @@
         return terms[0]
 
     me = lax.axis_index("expert").astype(jnp.int32).reshape(1)
+    others = planes - 1
+    sources = [gate_weights.T, expert_ids.T, segments, keep_counts, tokens, cotangent]
     routed = pl.pallas_call(
         functools.partial(route_kernel, planes, local),
-        out_shape=[jax.ShapeDtypeStruct((cap, width), low)] * (local * planes)
-        + [jax.ShapeDtypeStruct((local * cap, width), low)] * planes
+        out_shape=[jax.ShapeDtypeStruct((local * cap, width), low)] * 2
+        + [jax.ShapeDtypeStruct((cap, width), low)] * (local * others)
+        + [jax.ShapeDtypeStruct((local * cap, width), low)] * others
         + [
             jax.ShapeDtypeStruct((toks, top), jnp.int32),
             jax.ShapeDtypeStruct((toks, top), jnp.float32),
             jax.ShapeDtypeStruct((toks, 1), jnp.float32),
         ],
         in_specs=[pl.BlockSpec(memory_space=pltpu.SMEM)]
-        + [pl.BlockSpec(memory_space=pltpu.HBM)] * 2
-        + [pl.BlockSpec(memory_space=pltpu.VMEM)] * 4,
-        scratch_shapes=[
-            pltpu.VMEM(tokens.shape, tokens.dtype),
-            pltpu.VMEM(tokens.shape, tokens.dtype),
-            pltpu.SemaphoreType.DMA((2,)),
-        ],
+        + [pl.BlockSpec(memory_space=pltpu.HBM)] * len(sources),
+        scratch_shapes=[pltpu.VMEM(source.shape, source.dtype) for source in sources]
+        + [pltpu.SemaphoreType.DMA((len(sources),))],
         compiler_params=pltpu.CompilerParams(vmem_limit_bytes=40 << 20),
         name="route",
-    )(me, tokens, cotangent, gate_weights.T, expert_ids.T, segments, keep_counts)
+    )(me, *sources)
+    own_features, own_grads, *away = routed[:-3]
     target, weight, alive = routed[-3:]
     up_pair = swap(expand_weight, 1)
     down_pair = swap(reduce_weight, 1)
 
+    near_features = gather(own_features, order_of(0))
+    near_grads = gather(own_grads, order_of(1))
     features = []
     for l in range(local):
-        pieces = cross(routed[l * planes : (l + 1) * planes])
+        pieces = cross(away[l * others : (l + 1) * others])
         (own,) = run(
-            functools.partial(join_kernel, planes, cap), pieces, [((block_rows, width), low)]
-        )
-        features.append(gather(own, order_of(l)))
-    pieces = cross(routed[local * planes : (local + 1) * planes])
+            functools.partial(join_kernel, others, cap), pieces, [((others * cap, width), low)]
+        )
+        near = [(block, l, cap) for block in near_features]
+        features.append(near + gather(own, order_of(l)))
+    pieces = cross(away[local * others :])
     owns = run(
-        functools.partial(join_kernel, planes, cap), pieces, [((block_rows, width), low)] * local
-    )
-    grads = [gather(owns[l], order_of(l)) for l in range(local)]
+        functools.partial(join_kernel, others, cap), pieces, [((others * cap, width), low)] * local
+    )
+    grads = [
+        [(block, l, cap) for block in near_grads] + gather(owns[l], order_of(l))
+        for l in range(local)
+    ]
 
     rows = blocks * block_rows
-
-    def outs_of(parts):
-        return [
-            ((blocks // 2, stop - start, width), low) for start, stop, _ in parts for _ in range(2)
-        ]
-
-    hiddens, slopes, result_terms = [], [], []
+    flat = ((rows, 2 * units), low)
+    wide = ((rows, 2 * units), jnp.float32)
+
+    def outs_of(l, parts):
+        sizes = [(l + 1) * cap] + [stop - start for start, stop, _ in parts[1:]]
+        return [((blocks // 2, size, width), low) for size in sizes for _ in range(2)]
+
+    hiddens, slopes, result_terms, held = [], [], [], []
     for l in range(local):
-        parts = [part_of(0, block_rows, order_of(l))]
-        hidden, slope, send, keep = run(
-            functools.partial(forward_kernel, blocks, parts),
+        parts = [part_of(0, cap, order_of(1)), part_of(cap, block_rows, order_of(l))]
+        hidden, slope, *sends = run(
+            functools.partial(forward_kernel, blocks, parts, len(held)),
             features[l]
-            + [(expand_weight, l), (up_pair, l), (reduce_weight, l), (down_pair, l)],
-            [((rows, 2 * units), low), ((rows, 2 * units), jnp.float32)] + outs_of(parts),
+            + [(expand_weight, l), (up_pair, l), (reduce_weight, l), (down_pair, l)]
+            + held,
+            [flat, wide] + outs_of(l, parts),
         )
         hiddens.append(hidden)
         slopes.append(slope)
-        result_terms.append([scatter(send, keep, order_of(l))])
-    half = block_rows // 2
-    dpres, input_terms = [], []
+        held = sends[:2]
+        result_terms.append([scatter(sends[2], sends[3], order_of(l))])
+    near_results = scatter(*held, order_of(1))
+    half = cap + others * cap // 32 * 16
+    dpres, input_terms, held = [], [], []
     for l in range(local):
-        parts = [part_of(0, half, order_of(0)), part_of(half, block_rows, order_of(1))]
+        parts = [
+            part_of(0, cap, order_of(0)),
+            part_of(cap, half, order_of(0)),
+            part_of(half, block_rows, order_of(1)),
+        ]
         dpre, *sends = run(
-            functools.partial(backward_kernel, blocks, parts),
+            functools.partial(backward_kernel, blocks, parts, len(held)),
             grads[l]
-            + [(expand_weight, l), (up_pair, l), (reduce_weight, l), (down_pair, l), slopes[l]],
-            [((rows, 2 * units), low)] + outs_of(parts),
+            + [(expand_weight, l), (up_pair, l), (reduce_weight, l), (down_pair, l), slopes[l]]
+            + held,
+            [flat] + outs_of(l, parts),
         )
         dpres.append(dpre)
+        held = sends[:2]
         input_terms.append(
-            [scatter(sends[2 * index], sends[2 * index + 1], order_of(index)) for index in range(2)]
-        )
+            [scatter(*sends[2 * index + 2 : 2 * index + 4], order_of(index)) for index in range(2)]
+        )
+    near_inputs = scatter(*held, order_of(0))
     owns, pairs = [], []
     for l in range(local):
         own, pair = run(
@@ -398,20 +447,21 @@
         outs = run(
             functools.partial(finish_kernel, groups),
             [item for parts in terms_list for terms in parts for item in terms],
-            [((len(terms_list) * cap, width), low)] * planes,
+            [((len(terms_list) * cap, width), low)] * others,
         )
         return cross(outs)
 
     returned = finish(result_terms)
     output, gating_grad = run(
-        functools.partial(output_kernel, planes),
-        returned + [tokens, cotangent, target, weight, alive],
+        functools.partial(output_kernel, len(near_results)),
+        near_results + returned + [tokens, cotangent, target, weight, alive],
         [(tokens.shape, low), ((top, toks), jnp.float32)],
     )
     back = [finish([input_terms[l]]) for l in range(local)]
     (tokens_grad,) = run(
-        functools.partial(input_kernel, planes, local),
-        [back[l][s] for s in range(planes) for l in range(local)]
+        functools.partial(input_kernel, len(near_inputs)),
+        near_inputs
+        + [back[l][s] for s in range(others) for l in range(local)]
         + [tokens, cotangent, target, alive],
         [(tokens.shape, low)],
     )

time: 194 us -> 190 us (0.979)
  waiting for transfers between devices: 105 us -> 90.4 us
  starting transfers between devices: 53.8 us -> 64.4 us
    ppermute x28 -> x38, waiting for transfers between devices: 62.9 us -> 48.6 us  [swap(): return lax.ppermute(values, 'dp', [(i, i ^ mask) for i in range(groups)])]
    ppermute x28 -> x38, starting transfers between devices: 30 us -> 38.8 us  [swap(): return lax.ppermute(values, 'dp', [(i, i ^ mask) for i in range(groups)])]
    pallas_call x21 -> x23, Pallas kernels: 26.1 us -> 25.8 us  [run(): pl.pallas_call(kernel, out_shape=outs, grid=(1,), in_specs=specs, out_spe...]
    unnamed x22 -> x26, local copies, waits for them, and re-layouts: 6.06 us -> 6.07 us
  transfers between devices with their start and end apart: 46 -> 56, of which waited for: 22 -> 26; matrix products, arithmetic and copies ran while one was open for 0% -> 0% of each run, Pallas kernels for 13% -> 13%
where the time goes in v1:
time: 190 us; the launch traced here: 189 us
  waiting for transfers between devices  90.4 us (48%)
  starting transfers between devices  64.4 us (34%)
  Pallas kernels  27.4 us (14%)
  local copies, waits for them, and re-layouts  6.07 us (3%)
    ppermute x38, waiting for transfers between devices, swap(): return lax.ppermute(values, 'dp', [(i, i ^ mask) for i in range(groups)])  48.6 us
    ppermute x18, waiting for transfers between devices, cross(): lax.ppermute(piece, 'expert', [(i, i ^ s) for i in range(planes)])  41.8 us
    ppermute x38, starting transfers between devices, swap(): return lax.ppermute(values, 'dp', [(i, i ^ mask) for i in range(groups)])  38.8 us
    pallas_call x23, Pallas kernels, run(): pl.pallas_call(kernel, out_shape=outs, grid=(1,), in_specs=specs, out_spe...  25.8 us
    ppermute x18, starting transfers between devices, cross(): lax.ppermute(piece, 'expert', [(i, i ^ s) for i in range(planes)])  25.6 us
    unnamed x26, local copies, waits for them, and re-layouts  6.07 us
  transfers between devices with their start and end apart: 56, of which 26 were waited for; matrix products, arithmetic and copies ran while one was open for 0% of the time, Pallas kernels for 13%

profile of v1, /device:TPU:0, one launch (start us, length us, event | category | flops | bytes accessed | tf_op | source)
XLA Modules:
  0.0 189.1 jit_solution(15073873114795842842)
XLA Ops:
  5.9 1.6 route.1
  7.5 3.1 %collective-permute-start.3 = (bf16[32,1280]{1,0:T(8,128)(2,1)S(1)}, bf16[32,1280]{1,0:T(8,128)(2,1)S(1)}, u32[]{:S(2)}, u32[]{:S(2)}) collective-permute-start(bf16[32,1280]{1,0:T(8,128)(2,1)S(1)} %get-tuple-element.65), channel_id=1, source_target_pairs={{0,1},{1,0},{2,3},{3,2},{4,5},{5,4},{6,7},{7,6},{8,9},{9,8},{10,11... | collective-permute-start | bytes 245768 | tf_op jit(solution)/shard_map/ppermute | solution.py:305
  10.6 2.6 %collective-permute-start.4 = (bf16[32,1280]{1,0:T(8,128)(2,1)S(1)}, bf16[32,1280]{1,0:T(8,128)(2,1)S(1)}, u32[]{:S(2)}, u32[]{:S(2)}) collective-permute-start(bf16[32,1280]{1,0:T(8,128)(2,1)S(1)} %get-tuple-element.66), channel_id=1, source_target_pairs={{0,2},{1,3},{2,0},{3,1},{4,6},{5,7},{6,4},{7,5},{8,10},{9,11},{10,... | collective-permute-start | bytes 245768 | tf_op jit(solution)/shard_map/ppermute | solution.py:305
  13.3 1.8 collective-permute-start.11
  15.0 5.0 %collective-permute-done.4.refs_1_ = bf16[32,1280]{1,0:T(8,128)(2,1)S(1)} collective-permute-done((bf16[32,1280]{1,0:T(8,128)(2,1)S(1)}, bf16[32,1280]{1,0:T(8,128)(2,1)S(1)}, u32[]{:S(2)}, u32[]{:S(2)}) %collective-permute-start.4) | collective-permute-done | bytes 81952 | tf_op jit(solution)/shard_map/ppermute | solution.py:305
  20.0 1.5 collective-permute-start
  22.5 1.6 collective-permute-start.13
  24.1 5.0 %collective-permute-done.12.refs_1_ = bf16[32,1280]{1,0:T(8,128)(2,1)S(1)} collective-permute-done((bf16[32,1280]{1,0:T(8,128)(2,1)S(1)}, bf16[32,1280]{1,0:T(8,128)(2,1)S(1)}, u32[]{:S(2)}, u32[]{:S(2)}) %collective-permute-start.12) | collective-permute-done | bytes 81952 | tf_op jit(solution)/shard_map/ppermute | solution.py:305
  29.0 1.5 collective-permute-start.1
  31.8 2.6 %collective-permute-done.1.refs_2_ = bf16[64,1280]{1,0:T(8,128)(2,1)S(1)} collective-permute-done((bf16[64,1280]{1,0:T(8,128)(2,1)S(1)}, bf16[64,1280]{1,0:T(8,128)(2,1)S(1)}, u32[]{:S(2)}, u32[]{:S(2)}) %collective-permute-start.1) | collective-permute-done | bytes 163872 | tf_op jit(solution)/shard_map/ppermute | solution.py:300
  34.4 1.5 collective-permute-done.26.refs_1_.refs_9_
  36.7 2.5 %collective-permute-start.31 = (bf16[64,1280]{1,0:T(8,128)(2,1)S(1)}, bf16[64,1280]{1,0:T(8,128)(2,1)S(1)}, u32[]{:S(2)}, u32[]{:S(2)}) collective-permute-start(bf16[64,1280]{1,0:T(8,128)(2,1)S(1)} %get-tuple-element.89), channel_id=1, source_target_pairs={{0,3},{1,2},{2,1},{3,0},{4,7},{5,6},{6,5},{7,4},{8,11},{9,10},{10,... | collective-permute-start | bytes 491528 | tf_op jit(solution)/shard_map/ppermute | solution.py:305
  39.2 2.2 %collective-permute-done.29.refs_0_ = bf16[64,1280]{1,0:T(8,128)(2,1)S(1)} collective-permute-done((bf16[64,1280]{1,0:T(8,128)(2,1)S(1)}, bf16[64,1280]{1,0:T(8,128)(2,1)S(1)}, u32[]{:S(2)}, u32[]{:S(2)}) %collective-permute-start.29) | collective-permute-done | bytes 163872 | tf_op jit(solution)/shard_map/ppermute | solution.py:305
  42.9 3.6 %collective-permute-done.30.refs_1_ = bf16[64,1280]{1,0:T(8,128)(2,1)S(1)} collective-permute-done((bf16[64,1280]{1,0:T(8,128)(2,1)S(1)}, bf16[64,1280]{1,0:T(8,128)(2,1)S(1)}, u32[]{:S(2)}, u32[]{:S(2)}) %collective-permute-start.30) | collective-permute-done | bytes 163872 | tf_op jit(solution)/shard_map/ppermute | solution.py:305
  47.7 1.5 collective-permute-start.14
  49.3 4.3 %collective-permute-done.2.refs_3_ = bf16[64,1280]{1,0:T(8,128)(2,1)S(1)} collective-permute-done((bf16[64,1280]{1,0:T(8,128)(2,1)S(1)}, bf16[64,1280]{1,0:T(8,128)(2,1)S(1)}, u32[]{:S(2)}, u32[]{:S(2)}) %collective-permute-start.2) | collective-permute-done | bytes 163872 | tf_op jit(solution)/shard_map/ppermute | solution.py:300
  53.6 1.6 collective-permute-start.15
  56.9 5.5 %collective-permute-done.15.refs_6_ = bf16[96,1280]{1,0:T(8,128)(2,1)S(1)} collective-permute-done((bf16[96,1280]{1,0:T(8,128)(2,1)S(1)}, bf16[96,1280]{1,0:T(8,128)(2,1)S(1)}, u32[]{:S(2)}, u32[]{:S(2)}) %collective-permute-start.15) | collective-permute-done | bytes 245792 | tf_op jit(solution)/shard_map/ppermute | solution.py:300
  63.6 1.5 collective-permute-start.36
  65.1 2.6 %collective-permute-done.33.refs_6_.refs_14_ = bf16[96,1280]{1,0:T(8,128)(2,1)S(1)} collective-permute-done((bf16[96,1280]{1,0:T(8,128)(2,1)S(1)}, bf16[96,1280]{1,0:T(8,128)(2,1)S(1)}, u32[]{:S(2)}, u32[]{:S(2)}) %collective-permute-start.33) | collective-permute-done | bytes 245792 | tf_op jit(solution)/shard_map/ppermute | solution.py:300
  67.7 1.7 collective-permute-start.16
  69.3 1.9 %collective-permute-done.35.refs_5_.refs_13_ = bf16[96,1280]{1,0:T(8,128)(2,1)S(1)} collective-permute-done((bf16[96,1280]{1,0:T(8,128)(2,1)S(1)}, bf16[96,1280]{1,0:T(8,128)(2,1)S(1)}, u32[]{:S(2)}, u32[]{:S(2)}) %collective-permute-start.35) | collective-permute-done | bytes 245792 | tf_op jit(solution)/shard_map/ppermute | solution.py:300
  71.2 1.7 collective-permute-start.37
  78.6 3.7 %shard_map.121 = (bf16[512,640]{1,0:T(8,128)(2,1)S(1)}, f32[512,640]{1,0:T(8,128)S(1)}, bf16[2,32,1280]{2,1,0:T(8,128)(2,1)S(1)}, bf16[2,32,1280]{2,1,0:T(8,128)...) custom-call(bf16[64,1280]{1,0:T(8,128)(2,1)S(1)} %get-tuple-element.64.refs_0_, ...), custom_call_target="tpu_custom_call" | custom-call | tf_op jit(solution)/shard_map/pallas_call | solution.py:275
  82.3 4.4 %shard_map.129 = (bf16[512,640]{1,0:T(8,128)(2,1)S(1)}, bf16[2,32,1280]{2,1,0:T(8,128)(2,1)S(1)}, bf16[2,32,1280]{2,1,0:T(8,128)(2,1)S(1)}, bf16[2,48,1280]{2,1,...) custom-call(bf16[64,1280]{1,0:T(8,128)(2,1)S(1)} %get-tuple-element., ...), custom_call_target="tpu_custom_call" | custom-call | tf_op jit(solution)/shard_map/pallas_call | solution.py:275
  87.5 1.7 collective-permute-start.42
  89.2 3.6 %shard_map.122 = (bf16[512,640]{1,0:T(8,128)(2,1)S(1)}, f32[512,640]{1,0:T(8,128)S(1)}, bf16[2,64,1280]{2,1,0:T(8,128)(2,1)S(1)}, bf16[2,64,1280]{2,1,0:T(8,128)...) custom-call(bf16[64,1280]{1,0:T(8,128)(2,1)S(1)} %get-tuple-element.64.refs_0_, ...), custom_call_target="tpu_custom_call" | custom-call | tf_op jit(solution)/shard_map/pallas_call | solution.py:275
  92.8 4.2 %shard_map.130 = (bf16[512,640]{1,0:T(8,128)(2,1)S(1)}, bf16[2,64,1280]{2,1,0:T(8,128)(2,1)S(1)}, bf16[2,64,1280]{2,1,0:T(8,128)(2,1)S(1)}, bf16[2,48,1280]{2,1,...) custom-call(bf16[64,1280]{1,0:T(8,128)(2,1)S(1)} %get-tuple-element., ...), custom_call_target="tpu_custom_call" | custom-call | tf_op jit(solution)/shard_map/pallas_call | solution.py:275
  98.0 2.1 %shard_map.139 = (bf16[2,320,1280]{2,1,0:T(8,128)(2,1)S(1)}, bf16[2,320,1280]{2,1,0:T(8,128)(2,1)S(1)}) custom-call(bf16[64,1280]{1,0:T(8,128)(2,1)S(1)} %get-tuple-element.64.refs_0_, bf16[64,1280]{1,0:T(8,128)(2,1)S(1)} %collective-permute-done.refs_1_, bf16[64,1280]{1,0:T(8,128)(2,1)S(1)} %collective-permute-done.1.refs_2_, ...), custom_call_target="tpu_custom_call" | custom-call | tf_op jit(solution)/shard_map/pallas_call | solution.py:275
  100.2 1.9 %shard_map.140 = (bf16[2,320,1280]{2,1,0:T(8,128)(2,1)S(1)}, bf16[2,320,1280]{2,1,0:T(8,128)(2,1)S(1)}) custom-call(bf16[64,1280]{1,0:T(8,128)(2,1)S(1)} %get-tuple-element.64.refs_0_, bf16[64,1280]{1,0:T(8,128)(2,1)S(1)} %collective-permute-done.refs_1_, bf16[64,1280]{1,0:T(8,128)(2,1)S(1)} %collective-permute-done.1.refs_2_, ...), custom_call_target="tpu_custom_call" | custom-call | tf_op jit(solution)/shard_map/pallas_call | solution.py:275
  105.7 5.8 %collective-permute-done.47.refs_1_.refs_4_ = bf16[2,48,1280]{2,1,0:T(8,128)(2,1)S(1)} collective-permute-done((bf16[2,48,1280]{2,1,0:T(8,128)(2,1)S(1)}, bf16[2,48,1280]{2,1,0:T(8,128)(2,1)S(1)}, u32[]{:S(2)}, u32[]{:S(2)}) %collective-permute-start.47) | collective-permute-done | bytes 245792 | tf_op jit(solution)/shard_map/ppermute | solution.py:300
  112.7 5.9 %collective-permute-done.17.refs_1_ = bf16[2,64,1280]{2,1,0:T(8,128)(2,1)S(1)} collective-permute-done((bf16[2,64,1280]{2,1,0:T(8,128)(2,1)S(1)}, bf16[2,64,1280]{2,1,0:T(8,128)(2,1)S(1)}, u32[]{:S(2)}, u32[]{:S(2)}) %collective-permute-start.17) | collective-permute-done | bytes 327712 | tf_op jit(solution)/shard_map/ppermute | solution.py:300
  121.9 10.8 %collective-permute-done.43.refs_5_ = bf16[1,48,1280]{2,1,0:T(8,128)(2,1)S(1)} collective-permute-done((bf16[1,48,1280]{2,1,0:T(8,128)(2,1)S(1)}, bf16[1,48,1280]{2,1,0:T(8,128)(2,1)S(1)}, u32[]{:S(2)}, u32[]{:S(2)}) %collective-permute-start.43) | collective-permute-done | bytes 122912 | tf_op jit(solution)/shard_map/ppermute | solution.py:300
  133.8 3.7 %collective-permute-done.46.refs_2_ = bf16[1,48,1280]{2,1,0:T(8,128)(2,1)S(1)} collective-permute-done((bf16[1,48,1280]{2,1,0:T(8,128)(2,1)S(1)}, bf16[1,48,1280]{2,1,0:T(8,128)(2,1)S(1)}, u32[]{:S(2)}, u32[]{:S(2)}) %collective-permute-start.46) | collective-permute-done | bytes 122912 | tf_op jit(solution)/shard_map/ppermute | solution.py:300
  138.6 3.8 %collective-permute-done.48.refs_5_ = bf16[1,48,1280]{2,1,0:T(8,128)(2,1)S(1)} collective-permute-done((bf16[1,48,1280]{2,1,0:T(8,128)(2,1)S(1)}, bf16[1,48,1280]{2,1,0:T(8,128)(2,1)S(1)}, u32[]{:S(2)}, u32[]{:S(2)}) %collective-permute-start.48) | collective-permute-done | bytes 122912 | tf_op jit(solution)/shard_map/ppermute | solution.py:300
  143.3 3.7 %collective-permute-done.44.refs_3_ = bf16[32,1280]{1,0:T(8,128)(2,1)S(1)} collective-permute-done((bf16[32,1280]{1,0:T(8,128)(2,1)S(1)}, bf16[32,1280]{1,0:T(8,128)(2,1)S(1)}, u32[]{:S(2)}, u32[]{:S(2)}) %collective-permute-start.44) | collective-permute-done | bytes 81952 | tf_op jit(solution)/shard_map/ppermute | solution.py:305
  147.8 1.6 collective-permute-start.50
  150.7 1.5 collective-permute-done.49.refs_4_
  152.3 1.9 collective-permute-done.50.refs_5_
  154.8 5.7 %collective-permute-done.51.refs_6_ = bf16[32,1280]{1,0:T(8,128)(2,1)S(1)} collective-permute-done((bf16[32,1280]{1,0:T(8,128)(2,1)S(1)}, bf16[32,1280]{1,0:T(8,128)(2,1)S(1)}, u32[]{:S(2)}, u32[]{:S(2)}) %collective-permute-start.51) | collective-permute-done | bytes 81952 | tf_op jit(solution)/shard_map/ppermute | solution.py:305
  160.6 1.6 collective-permute-start.52
  162.2 4.9 %collective-permute-done.52.refs_7_ = bf16[32,1280]{1,0:T(8,128)(2,1)S(1)} collective-permute-done((bf16[32,1280]{1,0:T(8,128)(2,1)S(1)}, bf16[32,1280]{1,0:T(8,128)(2,1)S(1)}, u32[]{:S(2)}, u32[]{:S(2)}) %collective-permute-start.52) | collective-permute-done | bytes 81952 | tf_op jit(solution)/shard_map/ppermute | solution.py:305
  167.1 1.5 collective-permute-start.39
  168.7 2.5 %collective-permute-start.53 = (bf16[32,1280]{1,0:T(8,128)(2,1)S(1)}, bf16[32,1280]{1,0:T(8,128)(2,1)S(1)}, u32[]{:S(2)}, u32[]{:S(2)}) collective-permute-start(bf16[32,1280]{1,0:T(8,128)(2,1)S(1)} %get-tuple-element.111), channel_id=1, source_target_pairs={{0,3},{1,2},{2,1},{3,0},{4,7},{5,6},{6,5},{7,4},{8,11},{9,10},{10,... | collective-permute-start | bytes 245768 | tf_op jit(solution)/shard_map/ppermute | solution.py:305
  171.4 3.7 %collective-permute-done.53.refs_8_ = bf16[32,1280]{1,0:T(8,128)(2,1)S(1)} collective-permute-done((bf16[32,1280]{1,0:T(8,128)(2,1)S(1)}, bf16[32,1280]{1,0:T(8,128)(2,1)S(1)}, u32[]{:S(2)}, u32[]{:S(2)}) %collective-permute-start.53) | collective-permute-done | bytes 81952 | tf_op jit(solution)/shard_map/ppermute | solution.py:305
  175.0 3.1 %collective-permute-start.24 = (bf16[64,1280]{1,0:T(8,128)(2,1)S(1)}, bf16[64,1280]{1,0:T(8,128)(2,1)S(1)}, u32[]{:S(2)}, u32[]{:S(2)}) collective-permute-start(bf16[64,1280]{1,0:T(8,128)(2,1)S(1)} %get-tuple-element.80), channel_id=1, source_target_pairs={{0,2},{1,3},{2,0},{3,1},{4,6},{5,7},{6,4},{7,5},{8,10},{9,11},{10,... | collective-permute-start | bytes 491528 | tf_op jit(solution)/shard_map/ppermute | solution.py:305
  183.2 2.1 %collective-permute-done.25.refs_5_ = bf16[64,1280]{1,0:T(8,128)(2,1)S(1)} collective-permute-done((bf16[64,1280]{1,0:T(8,128)(2,1)S(1)}, bf16[64,1280]{1,0:T(8,128)(2,1)S(1)}, u32[]{:S(2)}, u32[]{:S(2)}) %collective-permute-start.25) | collective-permute-done | bytes 163872 | tf_op jit(solution)/shard_map/ppermute | solution.py:305
  186.8 2.4 %shard_map.141 = (bf16[2,320,1280]{2,1,0:T(8,128)(2,1)}, bf16[2,320,1280]{2,1,0:T(8,128)(2,1)}) custom-call(bf16[2,320,1280]{2,1,0:T(8,128)(2,1)S(1)} %get-tuple-element.115.refs_0_, bf16[2,320,1280]{2,1,0:T(8,128)(2,1)S(1)} %get-tuple-element.118.refs_1_, bf16[2,320,1280]{2,1,0:T(8,128)(2,1)S(1)} %collective-permute-done.54.refs_2_, ...), custom_call_target="tpu_custom_call" | custom-call | tf_op jit(solution)/shard_map/pallas_call | solution.py:275
  (114 shorter events, 42.5 us)
Async XLA Ops:
  0.6 74.4 %collective-permute-start.9 = (bf16[2,320,1280]{2,1,0:T(8,128)(2,1)}, bf16[2,320,1280]{2,1,0:T(8,128)(2,1)S(1)}, u32[]{:S(2)}, u32[]{:S(2)}) collective-permute-start(bf16[2,320,1280]{2,1,0:T(8,128)(2,1)} %refs_8_.7), channel_id=1, source_target_pairs={{0,4},{4,0},{8,12},{12,8},{16,20},{20,16},{24,28},{28,24},{1,5},{5... | collective-permute-start | bytes 4915208 | tf_op jit(solution)/shard_map/ppermute | solution.py:300
  1.2 74.7 %collective-permute-start.10 = (bf16[2,320,1280]{2,1,0:T(8,128)(2,1)}, bf16[2,320,1280]{2,1,0:T(8,128)(2,1)}, u32[]{:S(2)}, u32[]{:S(2)}) collective-permute-start(bf16[2,320,1280]{2,1,0:T(8,128)(2,1)} %refs_10_.8), channel_id=1, source_target_pairs={{0,4},{4,0},{8,12},{12,8},{16,20},{20,16},{24,28},{28,24},{1,5},{5... | collective-permute-start | bytes 4915208 | tf_op jit(solution)/shard_map/ppermute | solution.py:300
  10.6 9.4 %collective-permute-start.4 = (bf16[32,1280]{1,0:T(8,128)(2,1)S(1)}, bf16[32,1280]{1,0:T(8,128)(2,1)S(1)}, u32[]{:S(2)}, u32[]{:S(2)}) collective-permute-start(bf16[32,1280]{1,0:T(8,128)(2,1)S(1)} %get-tuple-element.66), channel_id=1, source_target_pairs={{0,2},{1,3},{2,0},{3,1},{4,6},{5,7},{6,4},{7,5},{8,10},{9,11},{10,... | collective-permute-start | bytes 245768 | tf_op jit(solution)/shard_map/ppermute | solution.py:305
  13.2 8.3 %collective-permute-start.5 = (bf16[32,1280]{1,0:T(8,128)(2,1)S(1)}, bf16[32,1280]{1,0:T(8,128)(2,1)S(1)}, u32[]{:S(2)}, u32[]{:S(2)}) collective-permute-start(bf16[32,1280]{1,0:T(8,128)(2,1)S(1)} %get-tuple-element.67), channel_id=1, source_target_pairs={{0,3},{1,2},{2,1},{3,0},{4,7},{5,6},{6,5},{7,4},{8,11},{9,10},{10,... | collective-permute-start | bytes 245768 | tf_op jit(solution)/shard_map/ppermute | solution.py:305
  13.3 9.2 %collective-permute-start.11 = (bf16[32,1280]{1,0:T(8,128)(2,1)S(1)}, bf16[32,1280]{1,0:T(8,128)(2,1)S(1)}, u32[]{:S(2)}, u32[]{:S(2)}) collective-permute-start(bf16[32,1280]{1,0:T(8,128)(2,1)S(1)} %get-tuple-element.68), channel_id=1, source_target_pairs={{0,1},{1,0},{2,3},{3,2},{4,5},{5,4},{6,7},{7,6},{8,9},{9,8},{10,11... | collective-permute-start | bytes 245768 | tf_op jit(solution)/shard_map/ppermute | solution.py:305
  20.0 10.7 %collective-permute-start = (bf16[64,1280]{1,0:T(8,128)(2,1)S(1)}, bf16[64,1280]{1,0:T(8,128)(2,1)S(1)}, u32[]{:S(2)}, u32[]{:S(2)}) collective-permute-start(bf16[64,1280]{1,0:T(8,128)(2,1)S(1)} %get-tuple-element.64.refs_0_), channel_id=1, source_target_pairs={{0,8},{4,12},{8,0},{12,4},{16,24},{20,28},{24,16},{28,20},{1,9},{5... | collective-permute-start | bytes 491528 | tf_op jit(solution)/shard_map/ppermute | solution.py:300
  21.5 7.5 %collective-permute-start.12 = (bf16[32,1280]{1,0:T(8,128)(2,1)S(1)}, bf16[32,1280]{1,0:T(8,128)(2,1)S(1)}, u32[]{:S(2)}, u32[]{:S(2)}) collective-permute-start(bf16[32,1280]{1,0:T(8,128)(2,1)S(1)} %get-tuple-element.69), channel_id=1, source_target_pairs={{0,2},{1,3},{2,0},{3,1},{4,6},{5,7},{6,4},{7,5},{8,10},{9,11},{10,... | collective-permute-start | bytes 245768 | tf_op jit(solution)/shard_map/ppermute | solution.py:305
  22.5 8.1 %collective-permute-start.13 = (bf16[32,1280]{1,0:T(8,128)(2,1)S(1)}, bf16[32,1280]{1,0:T(8,128)(2,1)S(1)}, u32[]{:S(2)}, u32[]{:S(2)}) collective-permute-start(bf16[32,1280]{1,0:T(8,128)(2,1)S(1)} %get-tuple-element.70), channel_id=1, source_target_pairs={{0,3},{1,2},{2,1},{3,0},{4,7},{5,6},{6,5},{7,4},{8,11},{9,10},{10,... | collective-permute-start | bytes 245768 | tf_op jit(solution)/shard_map/ppermute | solution.py:305
  34.4 7.1 %collective-permute-start.29 = (bf16[64,1280]{1,0:T(8,128)(2,1)S(1)}, bf16[64,1280]{1,0:T(8,128)(2,1)S(1)}, u32[]{:S(2)}, u32[]{:S(2)}) collective-permute-start(bf16[64,1280]{1,0:T(8,128)(2,1)S(1)} %get-tuple-element.87), channel_id=1, source_target_pairs={{0,1},{1,0},{2,3},{3,2},{4,5},{5,4},{6,7},{7,6},{8,9},{9,8},{10,11... | collective-permute-start | bytes 491528 | tf_op jit(solution)/shard_map/ppermute | solution.py:305
  35.9 10.6 %collective-permute-start.30 = (bf16[64,1280]{1,0:T(8,128)(2,1)S(1)}, bf16[64,1280]{1,0:T(8,128)(2,1)S(1)}, u32[]{:S(2)}, u32[]{:S(2)}) collective-permute-start(bf16[64,1280]{1,0:T(8,128)(2,1)S(1)} %get-tuple-element.88), channel_id=1, source_target_pairs={{0,2},{1,3},{2,0},{3,1},{4,6},{5,7},{6,4},{7,5},{8,10},{9,11},{10,... | collective-permute-start | bytes 491528 | tf_op jit(solution)/shard_map/ppermute | solution.py:305
  36.7 11.0 %collective-permute-start.31 = (bf16[64,1280]{1,0:T(8,128)(2,1)S(1)}, bf16[64,1280]{1,0:T(8,128)(2,1)S(1)}, u32[]{:S(2)}, u32[]{:S(2)}) collective-permute-start(bf16[64,1280]{1,0:T(8,128)(2,1)S(1)} %get-tuple-element.89), channel_id=1, source_target_pairs={{0,3},{1,2},{2,1},{3,0},{4,7},{5,6},{6,5},{7,4},{8,11},{9,10},{10,... | collective-permute-start | bytes 491528 | tf_op jit(solution)/shard_map/ppermute | solution.py:305
  41.5 13.8 %collective-permute-start.7 = (bf16[96,1280]{1,0:T(8,128)(2,1)S(1)}, bf16[96,1280]{1,0:T(8,128)(2,1)S(1)}, u32[]{:S(2)}, u32[]{:S(2)}) collective-permute-start(bf16[96,1280]{1,0:T(8,128)(2,1)S(1)} %shard_map.119.refs_4_), channel_id=1, source_target_pairs={{0,16},{4,20},{8,24},{12,28},{16,0},{20,4},{24,8},{28,12},{1,17},{... | collective-permute-start | bytes 737288 | tf_op jit(solution)/shard_map/ppermute | solution.py:300
  46.5 7.1 %collective-permute-start.2 = (bf16[64,1280]{1,0:T(8,128)(2,1)S(1)}, bf16[64,1280]{1,0:T(8,128)(2,1)S(1)}, u32[]{:S(2)}, u32[]{:S(2)}) collective-permute-start(bf16[64,1280]{1,0:T(8,128)(2,1)S(1)} %collective-permute-done.refs_1_), channel_id=1, source_target_pairs={{0,16},{4,20},{8,24},{12,28},{16,0},{20,4},{24,8},{28,12},{1,17},{... | collective-permute-start | bytes 491528 | tf_op jit(solution)/shard_map/ppermute | solution.py:300
  47.7 8.0 %collective-permute-start.14 = (bf16[96,1280]{1,0:T(8,128)(2,1)S(1)}, bf16[96,1280]{1,0:T(8,128)(2,1)S(1)}, u32[]{:S(2)}, u32[]{:S(2)}) collective-permute-start(bf16[96,1280]{1,0:T(8,128)(2,1)S(1)} %shard_map.120.refs_4_), channel_id=1, source_target_pairs={{0,8},{4,12},{8,0},{12,4},{16,24},{20,28},{24,16},{28,20},{1,9},{5... | collective-permute-start | bytes 737288 | tf_op jit(solution)/shard_map/ppermute | solution.py:300
  53.6 8.8 %collective-permute-start.15 = (bf16[96,1280]{1,0:T(8,128)(2,1)S(1)}, bf16[96,1280]{1,0:T(8,128)(2,1)S(1)}, u32[]{:S(2)}, u32[]{:S(2)}) collective-permute-start(bf16[96,1280]{1,0:T(8,128)(2,1)S(1)} %shard_map.120.refs_4_), channel_id=1, source_target_pairs={{0,16},{4,20},{8,24},{12,28},{16,0},{20,4},{24,8},{28,12},{1,17},{... | collective-permute-start | bytes 737288 | tf_op jit(solution)/shard_map/ppermute | solution.py:300
  55.3 12.4 %collective-permute-start.33 = (bf16[96,1280]{1,0:T(8,128)(2,1)S(1)}, bf16[96,1280]{1,0:T(8,128)(2,1)S(1)}, u32[]{:S(2)}, u32[]{:S(2)}) collective-permute-start(bf16[96,1280]{1,0:T(8,128)(2,1)S(1)} %get-tuple-element.90.refs_4_.refs_12_), channel_id=1, source_target_pairs={{0,16},{4,20},{8,24},{12,28},{16,0},{20,4},{24,8},{28,12},{1,17},{... | collective-permute-start | bytes 737288 | tf_op jit(solution)/shard_map/ppermute | solution.py:300
  55.7 7.9 %collective-permute-start.28 = (bf16[64,1280]{1,0:T(8,128)(2,1)S(1)}, bf16[64,1280]{1,0:T(8,128)(2,1)S(1)}, u32[]{:S(2)}, u32[]{:S(2)}) collective-permute-start(bf16[64,1280]{1,0:T(8,128)(2,1)S(1)} %collective-permute-done.27.refs_2_.refs_10_), channel_id=1, source_target_pairs={{0,8},{4,12},{8,0},{12,4},{16,24},{20,28},{24,16},{28,20},{1,9},{5... | collective-permute-start | bytes 491528 | tf_op jit(solution)/shard_map/ppermute | solution.py:300
  62.4 8.8 %collective-permute-start.35 = (bf16[96,1280]{1,0:T(8,128)(2,1)S(1)}, bf16[96,1280]{1,0:T(8,128)(2,1)S(1)}, u32[]{:S(2)}, u32[]{:S(2)}) collective-permute-start(bf16[96,1280]{1,0:T(8,128)(2,1)S(1)} %get-tuple-element.92.refs_4_.refs_12_), channel_id=1, source_target_pairs={{0,8},{4,12},{8,0},{12,4},{16,24},{20,28},{24,16},{28,20},{1,9},{5... | collective-permute-start | bytes 737288 | tf_op jit(solution)/shard_map/ppermute | solution.py:300
  63.6 9.3 %collective-permute-start.36 = (bf16[96,1280]{1,0:T(8,128)(2,1)S(1)}, bf16[96,1280]{1,0:T(8,128)(2,1)S(1)}, u32[]{:S(2)}, u32[]{:S(2)}) collective-permute-start(bf16[96,1280]{1,0:T(8,128)(2,1)S(1)} %get-tuple-element.92.refs_4_.refs_12_), channel_id=1, source_target_pairs={{0,16},{4,20},{8,24},{12,28},{16,0},{20,4},{24,8},{28,12},{1,17},{... | collective-permute-start | bytes 737288 | tf_op jit(solution)/shard_map/ppermute | solution.py:300
  67.7 6.2 %collective-permute-start.16 = (bf16[96,1280]{1,0:T(8,128)(2,1)S(1)}, bf16[96,1280]{1,0:T(8,128)(2,1)S(1)}, u32[]{:S(2)}, u32[]{:S(2)}) collective-permute-start(bf16[96,1280]{1,0:T(8,128)(2,1)S(1)} %collective-permute-done.14.refs_5_), channel_id=1, source_target_pairs={{0,16},{4,20},{8,24},{12,28},{16,0},{20,4},{24,8},{28,12},{1,17},{... | collective-permute-start | bytes 737288 | tf_op jit(solution)/shard_map/ppermute | solution.py:300
  71.2 11.0 %collective-permute-start.37 = (bf16[96,1280]{1,0:T(8,128)(2,1)S(1)}, bf16[96,1280]{1,0:T(8,128)(2,1)S(1)}, u32[]{:S(2)}, u32[]{:S(2)}) collective-permute-start(bf16[96,1280]{1,0:T(8,128)(2,1)S(1)} %collective-permute-done.35.refs_5_.refs_13_), channel_id=1, source_target_pairs={{0,16},{4,20},{8,24},{12,28},{16,0},{20,4},{24,8},{28,12},{1,17},{... | collective-permute-start | bytes 737288 | tf_op jit(solution)/shard_map/ppermute | solution.py:300
  72.9 14.6 %collective-permute-start.6 = (bf16[96,1280]{1,0:T(8,128)(2,1)S(1)}, bf16[96,1280]{1,0:T(8,128)(2,1)S(1)}, u32[]{:S(2)}, u32[]{:S(2)}) collective-permute-start(bf16[96,1280]{1,0:T(8,128)(2,1)S(1)} %shard_map.119.refs_4_), channel_id=1, source_target_pairs={{0,8},{4,12},{8,0},{12,4},{16,24},{20,28},{24,16},{28,20},{1,9},{5... | collective-permute-start | bytes 737288 | tf_op jit(solution)/shard_map/ppermute | solution.py:300
  73.9 15.3 %collective-permute-start.8 = (bf16[96,1280]{1,0:T(8,128)(2,1)S(1)}, bf16[96,1280]{1,0:T(8,128)(2,1)S(1)}, u32[]{:S(2)}, u32[]{:S(2)}) collective-permute-start(bf16[96,1280]{1,0:T(8,128)(2,1)S(1)} %collective-permute-done.7.refs_6_), channel_id=1, source_target_pairs={{0,8},{4,12},{8,0},{12,4},{16,24},{20,28},{24,16},{28,20},{1,9},{5... | collective-permute-start | bytes 737288 | tf_op jit(solution)/shard_map/ppermute | solution.py:300
  75.1 17.7 %collective-permute-start.32 = (bf16[96,1280]{1,0:T(8,128)(2,1)S(1)}, bf16[96,1280]{1,0:T(8,128)(2,1)S(1)}, u32[]{:S(2)}, u32[]{:S(2)}) collective-permute-start(bf16[96,1280]{1,0:T(8,128)(2,1)S(1)} %get-tuple-element.90.refs_4_.refs_12_), channel_id=1, source_target_pairs={{0,8},{4,12},{8,0},{12,4},{16,24},{20,28},{24,16},{28,20},{1,9},{5... | collective-permute-start | bytes 737288 | tf_op jit(solution)/shard_map/ppermute | solution.py:300
  75.9 16.9 %collective-permute-start.34 = (bf16[96,1280]{1,0:T(8,128)(2,1)S(1)}, bf16[96,1280]{1,0:T(8,128)(2,1)S(1)}, u32[]{:S(2)}, u32[]{:S(2)}) collective-permute-start(bf16[96,1280]{1,0:T(8,128)(2,1)S(1)} %collective-permute-done.33.refs_6_.refs_14_), channel_id=1, source_target_pairs={{0,8},{4,12},{8,0},{12,4},{16,24},{20,28},{24,16},{28,20},{1,9},{5... | collective-permute-start | bytes 737288 | tf_op jit(solution)/shard_map/ppermute | solution.py:300
  86.7 16.0 %collective-permute-start.40 = (bf16[2,48,1280]{2,1,0:T(8,128)(2,1)}, bf16[2,48,1280]{2,1,0:T(8,128)(2,1)S(1)}, u32[]{:S(2)}, u32[]{:S(2)}) collective-permute-start(bf16[2,48,1280]{2,1,0:T(8,128)(2,1)} %get-tuple-element.99), channel_id=1, source_target_pairs={{0,8},{4,12},{8,0},{12,4},{16,24},{20,28},{24,16},{28,20},{1,9},{5... | collective-permute-start | bytes 737288 | tf_op jit(solution)/shard_map/ppermute | solution.py:300
  87.5 16.3 %collective-permute-start.42 = (bf16[2,48,1280]{2,1,0:T(8,128)(2,1)}, bf16[2,48,1280]{2,1,0:T(8,128)(2,1)S(1)}, u32[]{:S(2)}, u32[]{:S(2)}) collective-permute-start(bf16[2,48,1280]{2,1,0:T(8,128)(2,1)} %get-tuple-element.101), channel_id=1, source_target_pairs={{0,16},{4,20},{8,24},{12,28},{16,0},{20,4},{24,8},{28,12},{1,17},{... | collective-permute-start | bytes 737288 | tf_op jit(solution)/shard_map/ppermute | solution.py:300
  97.0 7.7 %collective-permute-start.45 = (bf16[2,48,1280]{2,1,0:T(8,128)(2,1)}, bf16[2,48,1280]{2,1,0:T(8,128)(2,1)S(1)}, u32[]{:S(2)}, u32[]{:S(2)}) collective-permute-start(bf16[2,48,1280]{2,1,0:T(8,128)(2,1)} %get-tuple-element.104), channel_id=1, source_target_pairs={{0,8},{4,12},{8,0},{12,4},{16,24},{20,28},{24,16},{28,20},{1,9},{5... | collective-permute-start | bytes 737288 | tf_op jit(solution)/shard_map/ppermute | solution.py:300
  100.1 86.6 %collective-permute-start.54 = (bf16[2,320,1280]{2,1,0:T(8,128)(2,1)S(1)}, bf16[2,320,1280]{2,1,0:T(8,128)(2,1)S(1)}, u32[]{:S(2)}, u32[]{:S(2)}) collective-permute-start(bf16[2,320,1280]{2,1,0:T(8,128)(2,1)S(1)} %get-tuple-element.119), channel_id=1, source_target_pairs={{0,4},{4,0},{8,12},{12,8},{16,20},{20,16},{24,28},{28,24},{1,5},{5... | collective-permute-start | bytes 4915208 | tf_op jit(solution)/shard_map/ppermute | solution.py:300
  102.1 84.6 %collective-permute-start.55 = (bf16[2,320,1280]{2,1,0:T(8,128)(2,1)S(1)}, bf16[2,320,1280]{2,1,0:T(8,128)(2,1)S(1)}, u32[]{:S(2)}, u32[]{:S(2)}) collective-permute-start(bf16[2,320,1280]{2,1,0:T(8,128)(2,1)S(1)} %get-tuple-element.120), channel_id=1, source_target_pairs={{0,4},{4,0},{8,12},{12,8},{16,20},{20,16},{24,28},{28,24},{1,5},{5... | collective-permute-start | bytes 4915208 | tf_op jit(solution)/shard_map/ppermute | solution.py:300
  102.7 8.8 %collective-permute-start.47 = (bf16[2,48,1280]{2,1,0:T(8,128)(2,1)S(1)}, bf16[2,48,1280]{2,1,0:T(8,128)(2,1)S(1)}, u32[]{:S(2)}, u32[]{:S(2)}) collective-permute-start(bf16[2,48,1280]{2,1,0:T(8,128)(2,1)S(1)} %get-tuple-element.106), channel_id=1, source_target_pairs={{0,16},{4,20},{8,24},{12,28},{16,0},{20,4},{24,8},{28,12},{1,17},{... | collective-permute-start | bytes 737288 | tf_op jit(solution)/shard_map/ppermute | solution.py:300
  103.8 14.7 %collective-permute-start.17 = (bf16[2,64,1280]{2,1,0:T(8,128)(2,1)S(1)}, bf16[2,64,1280]{2,1,0:T(8,128)(2,1)S(1)}, u32[]{:S(2)}, u32[]{:S(2)}) collective-permute-start(bf16[2,64,1280]{2,1,0:T(8,128)(2,1)S(1)} %get-tuple-element.74), channel_id=1, source_target_pairs={{0,16},{4,20},{8,24},{12,28},{16,0},{20,4},{24,8},{28,12},{1,17},{... | collective-permute-start | bytes 983048 | tf_op jit(solution)/shard_map/ppermute | solution.py:300
  104.7 14.8 %collective-permute-start.38 = (bf16[2,64,1280]{2,1,0:T(8,128)(2,1)S(1)}, bf16[2,64,1280]{2,1,0:T(8,128)(2,1)S(1)}, u32[]{:S(2)}, u32[]{:S(2)}) collective-permute-start(bf16[2,64,1280]{2,1,0:T(8,128)(2,1)S(1)} %get-tuple-element.97), channel_id=1, source_target_pairs={{0,8},{4,12},{8,0},{12,4},{16,24},{20,28},{24,16},{28,20},{1,9},{5... | collective-permute-start | bytes 983048 | tf_op jit(solution)/shard_map/ppermute | solution.py:300
  111.5 9.1 %collective-permute-start.41 = (bf16[1,48,1280]{2,1,0:T(8,128)(2,1)S(1)}, bf16[1,48,1280]{2,1,0:T(8,128)(2,1)S(1)}, u32[]{:S(2)}, u32[]{:S(2)}) collective-permute-start(bf16[1,48,1280]{2,1,0:T(8,128)(2,1)S(1)} %shard_map.132), channel_id=1, source_target_pairs={{0,16},{4,20},{8,24},{12,28},{16,0},{20,4},{24,8},{28,12},{1,17},{... | collective-permute-start | bytes 368648 | tf_op jit(solution)/shard_map/ppermute | solution.py:300
  118.5 29.3 %collective-permute-start.19 = (bf16[2,96,1280]{2,1,0:T(8,128)(2,1)S(1)}, bf16[2,96,1280]{2,1,0:T(8,128)(2,1)S(1)}, u32[]{:S(2)}, u32[]{:S(2)}) collective-permute-start(bf16[2,96,1280]{2,1,0:T(8,128)(2,1)S(1)} %copy-done.12), channel_id=1, source_target_pairs={{0,8},{4,12},{8,0},{12,4},{16,24},{20,28},{24,16},{28,20},{1,9},{5... | collective-permute-start | bytes 1474568 | tf_op jit(solution)/shard_map/ppermute | solution.py:300
  119.5 29.9 %collective-permute-start.21 = (bf16[2,96,1280]{2,1,0:T(8,128)(2,1)S(1)}, bf16[2,96,1280]{2,1,0:T(8,128)(2,1)S(1)}, u32[]{:S(2)}, u32[]{:S(2)}) collective-permute-start(bf16[2,96,1280]{2,1,0:T(8,128)(2,1)S(1)} %get-tuple-element.78), channel_id=1, source_target_pairs={{0,16},{4,20},{8,24},{12,28},{16,0},{20,4},{24,8},{28,12},{1,17},{... | collective-permute-start | bytes 1474568 | tf_op jit(solution)/shard_map/ppermute | solution.py:300
  120.7 12.0 %collective-permute-start.43 = (bf16[1,48,1280]{2,1,0:T(8,128)(2,1)S(1)}, bf16[1,48,1280]{2,1,0:T(8,128)(2,1)S(1)}, u32[]{:S(2)}, u32[]{:S(2)}) collective-permute-start(bf16[1,48,1280]{2,1,0:T(8,128)(2,1)S(1)} %shard_map.133), channel_id=1, source_target_pairs={{0,8},{4,12},{8,0},{12,4},{16,24},{20,28},{24,16},{28,20},{1,9},{5... | collective-permute-start | bytes 368648 | tf_op jit(solution)/shard_map/ppermute | solution.py:300
  147.8 6.3 %collective-permute-start.50 = (bf16[32,1280]{1,0:T(8,128)(2,1)S(1)}, bf16[32,1280]{1,0:T(8,128)(2,1)S(1)}, u32[]{:S(2)}, u32[]{:S(2)}) collective-permute-start(bf16[32,1280]{1,0:T(8,128)(2,1)S(1)} %get-tuple-element.108), channel_id=1, source_target_pairs={{0,2},{1,3},{2,0},{3,1},{4,6},{5,7},{6,4},{7,5},{8,10},{9,11},{10,... | collective-permute-start | bytes 245768 | tf_op jit(solution)/shard_map/ppermute | solution.py:305
  149.5 17.7 %collective-permute-start.20 = (bf16[1,96,1280]{2,1,0:T(8,128)(2,1)S(1)}, bf16[1,96,1280]{2,1,0:T(8,128)(2,1)S(1)}, u32[]{:S(2)}, u32[]{:S(2)}) collective-permute-start(bf16[1,96,1280]{2,1,0:T(8,128)(2,1)S(1)} %shard_map.124), channel_id=1, source_target_pairs={{0,16},{4,20},{8,24},{12,28},{16,0},{20,4},{24,8},{28,12},{1,17},{... | collective-permute-start | bytes 737288 | tf_op jit(solution)/shard_map/ppermute | solution.py:300
  152.2 16.5 %collective-permute-start.22 = (bf16[1,96,1280]{2,1,0:T(8,128)(2,1)S(1)}, bf16[1,96,1280]{2,1,0:T(8,128)(2,1)S(1)}, u32[]{:S(2)}, u32[]{:S(2)}) collective-permute-start(bf16[1,96,1280]{2,1,0:T(8,128)(2,1)S(1)} %shard_map.125), channel_id=1, source_target_pairs={{0,8},{4,12},{8,0},{12,4},{16,24},{20,28},{24,16},{28,20},{1,9},{5... | collective-permute-start | bytes 737288 | tf_op jit(solution)/shard_map/ppermute | solution.py:300
  154.1 6.4 %collective-permute-start.51 = (bf16[32,1280]{1,0:T(8,128)(2,1)S(1)}, bf16[32,1280]{1,0:T(8,128)(2,1)S(1)}, u32[]{:S(2)}, u32[]{:S(2)}) collective-permute-start(bf16[32,1280]{1,0:T(8,128)(2,1)S(1)} %get-tuple-element.109), channel_id=1, source_target_pairs={{0,2},{1,3},{2,0},{3,1},{4,6},{5,7},{6,4},{7,5},{8,10},{9,11},{10,... | collective-permute-start | bytes 245768 | tf_op jit(solution)/shard_map/ppermute | solution.py:305
  160.6 6.5 %collective-permute-start.52 = (bf16[32,1280]{1,0:T(8,128)(2,1)S(1)}, bf16[32,1280]{1,0:T(8,128)(2,1)S(1)}, u32[]{:S(2)}, u32[]{:S(2)}) collective-permute-start(bf16[32,1280]{1,0:T(8,128)(2,1)S(1)} %get-tuple-element.110), channel_id=1, source_target_pairs={{0,3},{1,2},{2,1},{3,0},{4,7},{5,6},{6,5},{7,4},{8,11},{9,10},{10,... | collective-permute-start | bytes 245768 | tf_op jit(solution)/shard_map/ppermute | solution.py:305
  167.1 8.0 %collective-permute-start.18 = (bf16[1,64,1280]{2,1,0:T(8,128)(2,1)S(1)}, bf16[1,64,1280]{2,1,0:T(8,128)(2,1)S(1)}, u32[]{:S(2)}, u32[]{:S(2)}) collective-permute-start(bf16[1,64,1280]{2,1,0:T(8,128)(2,1)S(1)} %shard_map.123), channel_id=1, source_target_pairs={{0,8},{4,12},{8,0},{12,4},{16,24},{20,28},{24,16},{28,20},{1,9},{5... | collective-permute-start | bytes 491528 | tf_op jit(solution)/shard_map/ppermute | solution.py:300
  167.1 11.0 %collective-permute-start.39 = (bf16[1,64,1280]{2,1,0:T(8,128)(2,1)S(1)}, bf16[1,64,1280]{2,1,0:T(8,128)(2,1)S(1)}, u32[]{:S(2)}, u32[]{:S(2)}) collective-permute-start(bf16[1,64,1280]{2,1,0:T(8,128)(2,1)S(1)} %shard_map.131), channel_id=1, source_target_pairs={{0,16},{4,20},{8,24},{12,28},{16,0},{20,4},{24,8},{28,12},{1,17},{... | collective-permute-start | bytes 491528 | tf_op jit(solution)/shard_map/ppermute | solution.py:300
  168.7 6.3 %collective-permute-start.53 = (bf16[32,1280]{1,0:T(8,128)(2,1)S(1)}, bf16[32,1280]{1,0:T(8,128)(2,1)S(1)}, u32[]{:S(2)}, u32[]{:S(2)}) collective-permute-start(bf16[32,1280]{1,0:T(8,128)(2,1)S(1)} %get-tuple-element.111), channel_id=1, source_target_pairs={{0,3},{1,2},{2,1},{3,0},{4,7},{5,6},{6,5},{7,4},{8,11},{9,10},{10,... | collective-permute-start | bytes 245768 | tf_op jit(solution)/shard_map/ppermute | solution.py:305
  175.0 6.7 %collective-permute-start.23 = (bf16[64,1280]{1,0:T(8,128)(2,1)S(1)}, bf16[64,1280]{1,0:T(8,128)(2,1)S(1)}, u32[]{:S(2)}, u32[]{:S(2)}) collective-permute-start(bf16[64,1280]{1,0:T(8,128)(2,1)S(1)} %get-tuple-element.79), channel_id=1, source_target_pairs={{0,1},{1,0},{2,3},{3,2},{4,5},{5,4},{6,7},{7,6},{8,9},{9,8},{10,11... | collective-permute-start | bytes 491528 | tf_op jit(solution)/shard_map/ppermute | solution.py:305
  175.0 8.2 %collective-permute-start.24 = (bf16[64,1280]{1,0:T(8,128)(2,1)S(1)}, bf16[64,1280]{1,0:T(8,128)(2,1)S(1)}, u32[]{:S(2)}, u32[]{:S(2)}) collective-permute-start(bf16[64,1280]{1,0:T(8,128)(2,1)S(1)} %get-tuple-element.80), channel_id=1, source_target_pairs={{0,2},{1,3},{2,0},{3,1},{4,6},{5,7},{6,4},{7,5},{8,10},{9,11},{10,... | collective-permute-start | bytes 491528 | tf_op jit(solution)/shard_map/ppermute | solution.py:305
  178.1 7.2 %collective-permute-start.25 = (bf16[64,1280]{1,0:T(8,128)(2,1)S(1)}, bf16[64,1280]{1,0:T(8,128)(2,1)S(1)}, u32[]{:S(2)}, u32[]{:S(2)}) collective-permute-start(bf16[64,1280]{1,0:T(8,128)(2,1)S(1)} %get-tuple-element.81), channel_id=1, source_target_pairs={{0,3},{1,2},{2,1},{3,0},{4,7},{5,6},{6,5},{7,4},{8,11},{9,10},{10,... | collective-permute-start | bytes 491528 | tf_op jit(solution)/shard_map/ppermute | solution.py:305
  (21 other events, 175.7 us)
